TPU v7x, 512 devices: a whole 4x8x8 slice. The times are simulated.
512 devices in a mesh: rng: 32 (over y, x), xr: 16 (over z, core).
Axes of the slice: x: 4, y: 8, z: 8, core: 2. Of those that a mesh axis runs over, the one named last changes fastest.
Arguments:
- incident: float32 [4, 512, 2048], P(None, 'rng', 'xr'), may hold values from -6 to 6
- inverse_diag: float32 [4, 512, 2048], P(None, 'rng', 'xr'), may hold values from -4 to 4
- previous: float32 [4, 512, 2048], P(None, 'rng', 'xr'), may hold values from -4 to 4
- heights: float32 [512, 2048], P('rng', 'xr'), may hold values from -3 to 3
- neighbours: int32 [24, 512, 2048], P(None, 'rng', 'xr'), may hold values from 0 to 47, as said below
- counts: int32 [512, 2048], P('rng', 'xr'), may hold values from 1 to 24
- transmit: float32 [32, 2, 64], P('rng'), may hold values from 0.02 to 1
- angle_weights: float32 [2, 2, 64], replicated, may hold values from -0.15 to 0.15
Outputs:
- forward_currents: float32 [4, 512, 2048], P(None, 'rng', 'xr')
- currents: float32 [4, 512, 2048], P(None, 'rng', 'xr')
Inputs may be any that keep to these rules, and one draw needn't show every extreme that they name: `neighbours`: the entries of one patch's list are distinct; slots at or beyond the patch's count hold entries that are not used.
All inputs are finite; a program needn't handle non-finite values.
Results may differ from a plain program's by a relative error of at most 0.0003.
Values sent between devices are 32-bit elements; how exact they have to be, the bound alone decides.
A program may use at most 128 MiB of HBM per device.

v0:
```python
import math

import jax
import jax.numpy as jnp
from jax import lax
from jax.sharding import PartitionSpec as P

F = 2
Q = 64
H = 3
LMAX = 24
OFFSETS = 48


green_scale = 0.25
phase_period = 64
highest_precision = lax.Precision.HIGHEST


def padded_2(block, sides, width):
    for axis, dim in sides:
        count = lax.axis_size(axis)
        forward = [(i, i + 1) for i in range(count - 1)]
        backward = [(target, source) for source, target in forward]
        low = lax.ppermute(
            lax.slice_in_dim(block, block.shape[dim] - width, None, axis=dim), axis, forward
        )
        high = lax.ppermute(lax.slice_in_dim(block, 0, width, axis=dim), axis, backward)
        block = jnp.concatenate([low, block, high], axis=dim)
    return block


def carried_in(value, axis, combine, identity, reverse):
    size, index = (lax.axis_size(axis), lax.axis_index(axis))
    everything = jax.tree.map(lambda part: lax.all_gather(part, axis), value)
    start = jax.tree.map(
        lambda part, zero: jnp.broadcast_to(jnp.asarray(zero, part.dtype), part.shape),
        value,
        identity,
    )

    def lap(k, before):
        at = size - 1 - k if reverse else k
        reached = at > index if reverse else at < index
        new = combine(before, jax.tree.map(lambda part: part[at], everything))
        return jax.tree.map(lambda a, b: jnp.where(reached, a, b), new, before)

    return lax.fori_loop(0, size, lap, start)


def wave_tables(frequency, direction, row_ids, col_ids, block_heights):
    angle_ids = jnp.arange(Q, dtype=jnp.int32)
    range_step = direction * (1 + angle_ids // 8 + 2 * frequency)
    cross_step = angle_ids % 8 - 4 + frequency
    height_lift = 0.3 + 0.2 * frequency + 0.03 * angle_ids.astype(jnp.float32)
    phase_turns = (
        range_step[:, None, None] * row_ids[None, :, None]
        + cross_step[:, None, None] * col_ids[None, None, :]
    ) % phase_period
    phase_angle = (
        phase_turns.astype(jnp.float32) * (2.0 * math.pi / phase_period)
        + height_lift[:, None, None] * block_heights[None]
    )
    return (jnp.cos(phase_angle), jnp.sin(phase_angle))


def static_offset(offset_code):
    full_code = offset_code + (1 if offset_code >= OFFSETS // 2 else 0)
    return (full_code // (2 * H + 1) - H, full_code % (2 * H + 1) - H)


def green_terms(distance, weight_live):
    pieces = []
    for frequency in range(F):
        wavenum = 0.5 * math.pi * (1.0 + 0.25 * frequency)
        magnitude = weight_live * green_scale / distance
        pieces.append(magnitude * jnp.cos(wavenum * distance))
        pieces.append(magnitude * jnp.sin(wavenum * distance))
    return jnp.stack(pieces)


def pair_product(left_pair, right_pair):
    return jnp.stack(
        [
            left_pair[0] * right_pair[0] - left_pair[1] * right_pair[1],
            left_pair[0] * right_pair[1] + left_pair[1] * right_pair[0],
        ]
    )


def complex_apply(coupling, values):
    pieces = []
    for frequency in range(F):
        pieces.append(
            pair_product(
                coupling[2 * frequency : 2 * frequency + 2],
                values[2 * frequency : 2 * frequency + 2],
            )
        )
    return jnp.concatenate(pieces, 0)


def coupling_matrix(wave_rows, inverse_pair):
    cos_rows = wave_rows[:Q]
    sin_rows = wave_rows[Q:]
    scaled = jnp.concatenate(
        [
            inverse_pair[0] * cos_rows - inverse_pair[1] * sin_rows,
            inverse_pair[0] * sin_rows + inverse_pair[1] * cos_rows,
        ],
        0,
    )
    products = jnp.einsum("ap,bp->ab", wave_rows, scaled, precision=highest_precision)
    real_part = products[:Q, :Q] + products[Q:, Q:]
    imag_part = products[:Q, Q:] - products[Q:, :Q]
    return jnp.stack([real_part, imag_part])


def project(wave_rows, values_pair):
    sums_both = jnp.einsum("ap,cp->ac", wave_rows, values_pair, precision=highest_precision)
    real_part = sums_both[:Q, 0] + sums_both[Q:, 1]
    imag_part = sums_both[:Q, 1] - sums_both[Q:, 0]
    return jnp.stack([real_part, imag_part])


def radiate(wave_rows, weights, carried, spread):
    real_s = carried[:Q]
    imag_s = carried[Q:]
    amp_real = weights[0] * real_s - weights[1] * imag_s
    amp_imag = weights[0] * imag_s + weights[1] * real_s
    mixing = jnp.stack(
        [jnp.concatenate([amp_real, -amp_imag]), jnp.concatenate([amp_imag, amp_real])]
    )
    return spread * jnp.dot(mixing, wave_rows, precision=highest_precision)


def affine_map(matrix_pair, source_pair, weights, decay, spread):
    kernel_real = matrix_pair[0] * weights[0][None, :] - matrix_pair[1] * weights[1][None, :]
    kernel_imag = matrix_pair[0] * weights[1][None, :] + matrix_pair[1] * weights[0][None, :]
    identity_q = jnp.eye(Q, dtype=jnp.float32)
    block_real = identity_q - spread * kernel_real
    block_imag = -spread * kernel_imag
    whole_block = jnp.concatenate(
        [
            jnp.concatenate([block_real, -block_imag], 1),
            jnp.concatenate([block_imag, block_real], 1),
        ],
        0,
    )
    decay_both = jnp.concatenate([decay, decay])
    return (
        decay_both[:, None] * whole_block,
        decay_both * jnp.concatenate([source_pair[0], source_pair[1]]),
    )


def compose(earlier, later):
    earlier_maps, earlier_shift = earlier
    later_maps, later_shift = later
    joined_maps = jnp.einsum("fij,fjk->fik", later_maps, earlier_maps, precision=highest_precision)
    joined_shift = (
        jnp.einsum("fij,fj->fi", later_maps, earlier_shift, precision=highest_precision)
        + later_shift
    )
    return (joined_maps, joined_shift)


def per_device(
    incident, inverse_diag, previous, heights, neighbours, counts, transmit, angle_weights
):
    rows_dev = incident.shape[1]
    cols_dev = incident.shape[2]
    patches = rows_dev * cols_dev
    block_id = lax.axis_index("rng")
    row_ids = block_id * rows_dev + jnp.arange(rows_dev, dtype=jnp.int32)
    col_ids = lax.axis_index("xr") * cols_dev + jnp.arange(cols_dev, dtype=jnp.int32)
    spread = 1.0 / math.sqrt(rows_dev * cols_dev * lax.axis_size("xr"))
    stacked = jnp.concatenate([previous, heights[None]], 0)
    padded = padded_2(stacked, (("rng", 1), ("xr", 2)), H)
    padded_heights = padded[2 * F]
    padded_old = padded[: 2 * F]
    slot_ids = jnp.arange(LMAX, dtype=jnp.int32)[:, None, None]
    live_slots = slot_ids < counts[None]

    def presence(offset_code):
        return jnp.sum(jnp.where(live_slots & (neighbours == offset_code), 1.0, 0.0), axis=0)

    def offset_coupling(offset_code):
        shift_row, shift_col = static_offset(offset_code)
        window = padded_heights[
            H + shift_row : H + shift_row + rows_dev, H + shift_col : H + shift_col + cols_dev
        ]
        distance = jnp.sqrt(
            float(shift_row * shift_row + shift_col * shift_col) + (window - heights) ** 2
        )
        return green_terms(distance, presence(offset_code))

    def field_window(padded_field, offset_code):
        shift_row, shift_col = static_offset(offset_code)
        return padded_field[
            :, H + shift_row : H + shift_row + rows_dev, H + shift_col : H + shift_col + cols_dev
        ]

    offset_table = [offset_coupling(offset_code) for offset_code in range(OFFSETS)]

    def near_field(padded_field):
        running = jnp.zeros((2 * F, rows_dev, cols_dev), jnp.float32)
        for offset_code in range(OFFSETS):
            running = running + complex_apply(
                offset_table[offset_code], field_window(padded_field, offset_code)
            )
        return running

    near_old = near_field(padded_old)
    inv_flat = inverse_diag.reshape(2 * F, patches)
    inc_flat = incident.reshape(2 * F, patches)
    old_flat = near_old.reshape(2 * F, patches)
    forward_waves = []
    backward_waves = []
    loaded = []
    matrix_list = []
    feed_list = []
    for frequency in range(F):
        cos_wave, sin_wave = wave_tables(frequency, 1, row_ids, col_ids, heights)
        forward_waves.append(jnp.concatenate([cos_wave, sin_wave], 0).reshape(2 * Q, patches))
        cos_wave, sin_wave = wave_tables(frequency, -1, row_ids, col_ids, heights)
        backward_waves.append(jnp.concatenate([cos_wave, sin_wave], 0).reshape(2 * Q, patches))
        inverse_pair = inv_flat[2 * frequency : 2 * frequency + 2]
        source_pair = pair_product(
            inverse_pair,
            inc_flat[2 * frequency : 2 * frequency + 2]
            - old_flat[2 * frequency : 2 * frequency + 2],
        )
        loaded.append(source_pair)
        matrix_list.append(
            jnp.stack(
                [
                    coupling_matrix(forward_waves[frequency], inverse_pair),
                    coupling_matrix(backward_waves[frequency], inverse_pair),
                ]
            )
        )
        feed_list.append(project(forward_waves[frequency], source_pair))
    local_mats = jnp.stack(matrix_list)
    local_feed = jnp.stack(feed_list)
    summed_mats, forward_feed = lax.psum((local_mats, local_feed), "xr")
    decay_rows = transmit[0]
    identity_maps = jnp.broadcast_to(jnp.eye(2 * Q, dtype=jnp.float32), (F, 2 * Q, 2 * Q))
    identity_shift = jnp.zeros((F, 2 * Q), jnp.float32)
    map_list = []
    shift_list = []
    for frequency in range(F):
        block_map, block_shift = affine_map(
            summed_mats[frequency, 0],
            forward_feed[frequency],
            angle_weights[frequency],
            decay_rows[frequency],
            spread,
        )
        map_list.append(block_map)
        shift_list.append(block_shift)
    forward_maps = jnp.stack(map_list)
    forward_shift = jnp.stack(shift_list)
    carry_forward = carried_in(
        (forward_maps, forward_shift), "rng", compose, (identity_maps, identity_shift), False
    )[1]
    weak_list = []
    flow_list = []
    for frequency in range(F):
        inverse_pair = inv_flat[2 * frequency : 2 * frequency + 2]
        weak_pair = radiate(
            forward_waves[frequency], angle_weights[frequency], carry_forward[frequency], spread
        )
        weak_list.append(weak_pair)
        flow_list.append(loaded[frequency] - pair_product(inverse_pair, weak_pair))
    forward_currents = jnp.concatenate(flow_list, 0).reshape(2 * F, rows_dev, cols_dev)
    padded_new = padded_2(forward_currents, (("rng", 1), ("xr", 2)), H)
    new_flat = near_field(padded_new).reshape(2 * F, patches)
    driven_list = []
    back_list = []
    for frequency in range(F):
        inverse_pair = inv_flat[2 * frequency : 2 * frequency + 2]
        rest_pair = (
            inc_flat[2 * frequency : 2 * frequency + 2]
            - new_flat[2 * frequency : 2 * frequency + 2]
            - weak_list[frequency]
        )
        driven_pair = pair_product(inverse_pair, rest_pair)
        driven_list.append(driven_pair)
        back_list.append(project(backward_waves[frequency], driven_pair))
    backward_feed = lax.psum(jnp.stack(back_list), "xr")
    map_list = []
    shift_list = []
    for frequency in range(F):
        block_map, block_shift = affine_map(
            summed_mats[frequency, 1],
            backward_feed[frequency],
            angle_weights[frequency],
            decay_rows[frequency],
            spread,
        )
        map_list.append(block_map)
        shift_list.append(block_shift)
    backward_maps = jnp.stack(map_list)
    backward_shift = jnp.stack(shift_list)
    carry_backward = carried_in(
        (backward_maps, backward_shift), "rng", compose, (identity_maps, identity_shift), True
    )[1]
    final_list = []
    for frequency in range(F):
        inverse_pair = inv_flat[2 * frequency : 2 * frequency + 2]
        weak_back = radiate(
            backward_waves[frequency], angle_weights[frequency], carry_backward[frequency], spread
        )
        final_list.append(driven_list[frequency] - pair_product(inverse_pair, weak_back))
    currents = jnp.concatenate(final_list, 0).reshape(2 * F, rows_dev, cols_dev)
    return (forward_currents, currents)


def solution(mesh):
    placed = (
        P(None, "rng", "xr"),
        P(None, "rng", "xr"),
        P(None, "rng", "xr"),
        P("rng", "xr"),
        P(None, "rng", "xr"),
        P("rng", "xr"),
        P("rng", None, None),
        P(),
    )
    return jax.shard_map(
        per_device,
        mesh=mesh,
        in_specs=placed,
        out_specs=(P(None, "rng", "xr"), P(None, "rng", "xr")),
        check_vma=False,
    )
```

profile of v0, /device:TPU:8, one launch (start us, length us, event | category | flops | bytes accessed | tf_op | source)
XLA Modules:
  0.0 451.9 jit_solution(11067108255347322339)
XLA Ops:
  8.6 4.5 %collective-permute-start.1 = (f32[5,3,128]{2,1,0:T(4,128)}, f32[5,3,128]{2,1,0:T(4,128)S(1)}, u32[]{:S(2)}, u32[]{:S(2)}) collective-permute-start(f32[5,3,128]{2,1,0:T(4,128)} %get-tuple-element.1329), channel_id=1, source_target_pairs={{16,0},{32,16},{48,32},{64,48},{80,64},{96,80},{112,96},{128,112},... | collective-permute-start | bytes 23048 | tf_op jit(solution)/shard_map/ppermute | solution.py:28
  13.1 1.9 collective-permute-start
  17.4 9.4 %multiply_subtract_fusion.3 = (f32[64,2048]{1,0:T(8,128)S(1)}, f32[64,2048]{1,0:T(8,128)S(1)}, f32[64,2048]{1,0:T(8,128)S(1)}, f32[64,2048]{1,0:T(8,128)S(1)}, f...) fusion(f32[2048]{0:T(1024)S(1)} %get-tuple-element.1354, ...), kind=kLoop, calls=%fused_computation.77 | loop fusion | flops 9175040 | bytes 8430080 | tf_op jit(solution)/shard_map/sub | solution.py:108
  34.0 3.8 select_reduce_fusion.47
  41.6 4.2 collective-permute-done.3
  47.6 1.6 subtract_bitcast_fusion.167
  50.7 1.6 subtract_bitcast_fusion.169
  52.3 1.6 subtract_bitcast_fusion.179
  53.8 1.6 subtract_bitcast_fusion.175
  55.5 1.6 subtract_bitcast_fusion.177
  57.1 1.6 subtract_bitcast_fusion.187
  58.7 1.6 subtract_bitcast_fusion.189
  60.3 1.5 subtract_bitcast_fusion.103
  61.8 1.5 subtract_bitcast_fusion.185
  66.2 1.6 subtract_bitcast_fusion.181
  70.7 1.5 subtract_bitcast_fusion.174
  72.2 1.5 subtract_bitcast_fusion.166
  74.4 1.5 subtract_bitcast_fusion.165
  78.1 1.5 subtract_bitcast_fusion.173
  86.6 66.6 %all-reduce.2.cloned.1.call-done = f32[2,2,2,64,64]{4,3,2,1,0:T(8,128)} async-done(((f32[2,2,2,64,64]{4,3,2,1,0:T(8,128)}), f32[2,2,2,64,64]{4,3,2,1,0:T(8,128)}) %all-reduce.2.cloned.1.call-update) | async-done | bytes 131088 | tf_op jit(solution)/shard_map/psum | solution.py:246
  178.0 2.0 fusion.142
  182.2 26.4 %psum.22 = f32[2,2,64]{2,1,0:T(2,128)S(1)} all-reduce(f32[2,2,64]{2,1,0:T(2,128)S(1)} %pad_maximum_fusion.34), channel_id=1, replica_groups=mesh['rng'=32,'xr'=16] {'xr'}, use_global_device_ids=true, to_apply=%region_49.50 | all-reduce | flops 256 | bytes 2048 | tf_op jit(solution)/shard_map/psum | solution.py:246
  210.3 38.5 %all-gather.4 = f32[32,2,128]{2,1,0:T(2,128)S(1)} all-gather(f32[1,2,128]{2,1,0:T(2,128)S(1)} %maximum_bitcast_fusion.16), channel_id=3, replica_groups=mesh['rng'=32,'xr'=16] {'rng'}, dimensions={0}, use_global_device_ids=true | all-gather | bytes 33792 | tf_op jit(solution)/shard_map/all_gather | solution.py:35
  248.8 1.6 pad_maximum_fusion.18
  250.6 40.4 %while.30 = (s32[]{:T(128)}, f32[2,128]{1,0:T(2,128)S(1)}, s32[]{:T(128)}, f32[32,2,128,128]{3,2,1,0:T(8,128)}, f32[32,2,128]{2,1,0:T(2,128)S(1)}, /*index=5*/s32[]{:T(128)}, s32[]{:T(128)}) while((s32[]{:T(128)}, f32[2,128]{1,0:T(2,128)S(1)}, s32[]{:T(128)}, f32[32,2,128,128]{3,2,1,0:T(8,128)}, f32[32,2,128]{2,1,0:T(2,128)S(1)}, ...), condition=%wide.region_51.52_spmd.clone, body=%wide.region_50.51_spmd.clone.sunk | while | flops 394244 | bytes 139378 | solution.py:48
  292.0 1.8 convolution_multiply_fusion.2
  294.7 4.1 collective-permute-start.5
  298.7 1.9 collective-permute-start.4
  301.3 5.2 %collective-permute-done.4 = f32[4,3,128]{2,1,0:T(4,128)S(1)} collective-permute-done((f32[4,3,128]{2,1,0:T(4,128)S(1)}, f32[4,3,128]{2,1,0:T(4,128)S(1)}, u32[]{:S(2)}, u32[]{:S(2)}) %collective-permute-start.4) | collective-permute-done | bytes 6176 | tf_op jit(solution)/shard_map/ppermute | solution.py:25
  337.3 25.4 %psum.23 = f32[2,2,64]{2,1,0:T(2,128)S(1)} all-reduce(f32[2,2,64]{2,1,0:T(2,128)S(1)} %pad_maximum_fusion.35), channel_id=1, replica_groups=mesh['rng'=32,'xr'=16] {'xr'}, use_global_device_ids=true, to_apply=%region_52.53 | all-reduce | flops 256 | bytes 2048 | tf_op jit(solution)/shard_map/psum | solution.py:291
  364.4 38.3 %all-gather.5 = f32[32,2,128]{2,1,0:T(2,128)S(1)} all-gather(f32[1,2,128]{2,1,0:T(2,128)S(1)} %maximum_bitcast_fusion.19), channel_id=5, replica_groups=mesh['rng'=32,'xr'=16] {'rng'}, dimensions={0}, use_global_device_ids=true | all-gather | bytes 33792 | tf_op jit(solution)/shard_map/all_gather | solution.py:35
  402.7 40.6 %while.31 = (s32[]{:T(128)}, f32[2,128]{1,0:T(2,128)S(1)}, s32[]{:T(128)}, f32[32,2,128,128]{3,2,1,0:T(8,128)}, f32[32,2,128]{2,1,0:T(2,128)S(1)}, /*index=5*/s32[]{:T(128)}, s32[]{:T(128)}, s32[]{:T(128)}, s32[]{:T(128)}) while((s32[]{:T(128)}, f32[2,128]{1,0:T(2,128)S(1)}, s32[]{:T(128)}, f32[32,2,128,128]{3,2,1,0:T(8,128)}, ...), condition=%wide.region_54.55_spmd.clone, body=%wide.region_53.54_spmd.clone.sunk | while | flops 394248 | bytes 139440 | solution.py:48
  (798 shorter events, 175.1 us)
Async XLA Ops:
  7.2 146.0 %all-reduce.2.cloned.1.call-start = ((), (), s32[]{:S(2)}) async-start(), calls=%async_computation | async-start | bytes 524288 | tf_op jit(solution)/shard_map/psum | solution.py:246
  8.6 30.1 %collective-permute-start.1 = (f32[5,3,128]{2,1,0:T(4,128)}, f32[5,3,128]{2,1,0:T(4,128)S(1)}, u32[]{:S(2)}, u32[]{:S(2)}) collective-permute-start(f32[5,3,128]{2,1,0:T(4,128)} %get-tuple-element.1329), channel_id=1, source_target_pairs={{16,0},{32,16},{48,32},{64,48},{80,64},{96,80},{112,96},{128,112},... | collective-permute-start | bytes 23048 | tf_op jit(solution)/shard_map/ppermute | solution.py:28
  13.1 25.6 %collective-permute-start = (f32[5,3,128]{2,1,0:T(4,128)S(1)}, f32[5,3,128]{2,1,0:T(4,128)S(1)}, u32[]{:S(2)}, u32[]{:S(2)}) collective-permute-start(f32[5,3,128]{2,1,0:T(4,128)S(1)} %get-tuple-element.1328), channel_id=1, source_target_pairs={{0,16},{16,32},{32,48},{48,64},{64,80},{80,96},{96,112},{112,128},... | collective-permute-start | bytes 23048 | tf_op jit(solution)/shard_map/ppermute | solution.py:25
  32.6 217.9 %all-gather.9.cloned.1.call-start = ((), (), s32[]{:S(2)}) async-start(), calls=%async_computation.1 | async-start | bytes 4325376 | tf_op jit(solution)/shard_map/all_gather | solution.py:35
  38.8 2.8 collective-permute-start.2
  40.3 5.6 %collective-permute-start.3 = (f32[5,22,3]{2,1,0:T(8,128)S(1)}, f32[5,22,3]{2,1,0:T(8,128)S(1)}, u32[]{:S(2)}, u32[]{:S(2)}) collective-permute-start(f32[5,22,3]{2,1,0:T(8,128)S(1)} %get-tuple-element.1305), channel_id=1, source_target_pairs={{1,0},{2,1},{3,2},{4,3},{5,4},{6,5},{7,6},{8,7},{9,8},{10,9},{11,1... | collective-permute-start | bytes 3968 | tf_op jit(solution)/shard_map/ppermute | solution.py:28
  158.5 244.1 %all-gather.11.cloned.1.call-start = ((), (), s32[]{:S(2)}) async-start(), calls=%async_computation.2 | async-start | bytes 4325376 | tf_op jit(solution)/shard_map/all_gather | solution.py:35
  162.2 88.3 %copy-start.15 = (f32[2,128]{1,0:T(2,128)S(1)}, f32[2,128]{1,0:T(2,128)}, u32[]{:S(2)}) copy-start(f32[2,128]{1,0:T(2,128)} %custom-call) | copy-start | bytes 3076
  171.3 122.5 %copy-start.9 = (f32[1,16,128]{2,1,0:T(8,128)S(1)}, f32[1,16,128]{2,1,0:T(8,128)}, u32[]{:S(2)}) copy-start(f32[1,16,128]{2,1,0:T(8,128)} %get-tuple-element.1358) | copy-start | bytes 24580
  171.3 122.5 %copy-start.11 = (f32[1,16,128]{2,1,0:T(8,128)S(1)}, f32[1,16,128]{2,1,0:T(8,128)}, u32[]{:S(2)}) copy-start(f32[1,16,128]{2,1,0:T(8,128)} %get-tuple-element.1359) | copy-start | bytes 24580
  176.5 118.1 %copy-start.7 = (f32[1,16,128]{2,1,0:T(8,128)S(1)}, f32[1,16,128]{2,1,0:T(8,128)}, u32[]{:S(2)}) copy-start(f32[1,16,128]{2,1,0:T(8,128)} %get-tuple-element.1357) | copy-start | bytes 24580
  181.0 141.3 %copy-start.99 = (f32[16,128]{1,0:T(8,128)S(1)}, f32[16,128]{1,0:T(8,128)}, u32[]{:S(2)}) copy-start(f32[16,128]{1,0:T(8,128)} %get-tuple-element.405) | copy-start | bytes 24580
  181.0 141.3 %copy-start.100 = (f32[16,128]{1,0:T(8,128)S(1)}, f32[16,128]{1,0:T(8,128)}, u32[]{:S(2)}) copy-start(f32[16,128]{1,0:T(8,128)} %get-tuple-element.406) | copy-start | bytes 24580
  182.1 147.2 %copy-start.76 = (f32[16,128]{1,0:T(8,128)S(1)}, f32[16,128]{1,0:T(8,128)}, u32[]{:S(2)}) copy-start(f32[16,128]{1,0:T(8,128)} %copy-done.75) | copy-start | bytes 24580
  182.1 147.2 %copy-start.78 = (f32[16,128]{1,0:T(8,128)S(1)}, f32[16,128]{1,0:T(8,128)}, u32[]{:S(2)}) copy-start(f32[16,128]{1,0:T(8,128)} %copy-done.77) | copy-start | bytes 24580
  182.1 148.1 %copy-start.72 = (f32[16,128]{1,0:T(8,128)S(1)}, f32[16,128]{1,0:T(8,128)}, u32[]{:S(2)}) copy-start(f32[16,128]{1,0:T(8,128)} %copy-done.71) | copy-start | bytes 24580
  182.1 148.1 %copy-start.74 = (f32[16,128]{1,0:T(8,128)S(1)}, f32[16,128]{1,0:T(8,128)}, u32[]{:S(2)}) copy-start(f32[16,128]{1,0:T(8,128)} %copy-done.73) | copy-start | bytes 24580
  250.5 83.3 %copy-start.66 = (f32[16,128]{1,0:T(8,128)S(1)}, f32[16,128]{1,0:T(8,128)}, u32[]{:S(2)}) copy-start(f32[16,128]{1,0:T(8,128)} %copy-done.65) | copy-start | bytes 24580
  250.6 83.3 %copy-start.68 = (f32[16,128]{1,0:T(8,128)S(1)}, f32[16,128]{1,0:T(8,128)}, u32[]{:S(2)}) copy-start(f32[16,128]{1,0:T(8,128)} %copy-done.67) | copy-start | bytes 24580
  250.6 83.3 %copy-start.69 = (f32[16,128]{1,0:T(8,128)S(1)}, f32[16,128]{1,0:T(8,128)}, u32[]{:S(2)}) copy-start(f32[16,128]{1,0:T(8,128)} %get-tuple-element.799) | copy-start | bytes 24580
  250.6 83.3 %copy-start.70 = (f32[16,128]{1,0:T(8,128)S(1)}, f32[16,128]{1,0:T(8,128)}, u32[]{:S(2)}) copy-start(f32[16,128]{1,0:T(8,128)} %get-tuple-element.800) | copy-start | bytes 24580
  250.6 83.3 %copy-start.88 = (f32[16,128]{1,0:T(8,128)S(1)}, f32[16,128]{1,0:T(8,128)}, u32[]{:S(2)}) copy-start(f32[16,128]{1,0:T(8,128)} %copy-done.87) | copy-start | bytes 24580
  250.6 83.4 %copy-start.62 = (f32[16,128]{1,0:T(8,128)S(1)}, f32[16,128]{1,0:T(8,128)}, u32[]{:S(2)}) copy-start(f32[16,128]{1,0:T(8,128)} %copy-done.61) | copy-start | bytes 24580
  250.6 83.4 %copy-start.64 = (f32[16,128]{1,0:T(8,128)S(1)}, f32[16,128]{1,0:T(8,128)}, u32[]{:S(2)}) copy-start(f32[16,128]{1,0:T(8,128)} %copy-done.63) | copy-start | bytes 24580
  250.6 83.4 %copy-start.92 = (f32[16,128]{1,0:T(8,128)S(1)}, f32[16,128]{1,0:T(8,128)}, u32[]{:S(2)}) copy-start(f32[16,128]{1,0:T(8,128)} %copy-done.91) | copy-start | bytes 24580
  250.6 83.4 %copy-start.94 = (f32[16,128]{1,0:T(8,128)S(1)}, f32[16,128]{1,0:T(8,128)}, u32[]{:S(2)}) copy-start(f32[16,128]{1,0:T(8,128)} %copy-done.93) | copy-start | bytes 24580
  294.7 6.6 %collective-permute-start.5 = (f32[4,3,128]{2,1,0:T(4,128)S(1)}, f32[4,3,128]{2,1,0:T(4,128)S(1)}, u32[]{:S(2)}, u32[]{:S(2)}) collective-permute-start(f32[4,3,128]{2,1,0:T(4,128)S(1)} %get-tuple-element.1345), channel_id=1, source_target_pairs={{16,0},{32,16},{48,32},{64,48},{80,64},{96,80},{112,96},{128,112},... | collective-permute-start | bytes 18440 | tf_op jit(solution)/shard_map/ppermute | solution.py:28
  298.7 7.8 %collective-permute-start.4 = (f32[4,3,128]{2,1,0:T(4,128)S(1)}, f32[4,3,128]{2,1,0:T(4,128)S(1)}, u32[]{:S(2)}, u32[]{:S(2)}) collective-permute-start(f32[4,3,128]{2,1,0:T(4,128)S(1)} %get-tuple-element.1344), channel_id=1, source_target_pairs={{0,16},{16,32},{32,48},{48,64},{64,80},{80,96},{96,112},{112,128},... | collective-permute-start | bytes 18440 | tf_op jit(solution)/shard_map/ppermute | solution.py:25
  308.2 4.2 collective-permute-start.6
  309.5 3.1 collective-permute-start.7
  314.5 88.2 %copy-start.14 = (f32[2,128]{1,0:T(2,128)S(1)}, f32[2,128]{1,0:T(2,128)}, u32[]{:S(2)}) copy-start(f32[2,128]{1,0:T(2,128)} %custom-call.1) | copy-start | bytes 3076
  324.1 119.1 %copy-start.203 = (f32[2,2,64]{2,1,0:T(2,128)S(1)}, f32[2,2,64]{2,1,0:T(2,128)}, u32[]{:S(2)}) copy-start(f32[2,2,64]{2,1,0:T(2,128)} %param.19) | copy-start | bytes 3076
  (185 other events, 4931.3 us)
Sparse Core Ops, SparseCore 0:
  32.7 120.3 all-reduce.1
  158.7 87.0 all-gather.8
  250.5 83.8 all-gather.10
where the time goes:
time: 460 us; the launch traced here: 452 us
  blocking collectives  129 us (28%)
  other arithmetic  117 us (25%)
  matrix products  89 us (19%)
  waiting for transfers between devices  76.3 us (17%)
  starting transfers between devices  18.3 us (4%)
  between operations  17.3 us (4%)
    another operation x82, other arithmetic, pair_product(): jnp.stack([left_pair[0] * right_pair[0] - left_pair[1] * right_pair[1], l...  80.5 us
    dot_general x64, matrix products, compose(): jnp.einsum('fij,fj->fi', later_maps, earlier_shift, precision=highest_pre...  77.8 us
    all_gather x2, blocking collectives, carried_in(): everything = jax.tree.map(lambda part: lax.all_gather(part, axis), value)  76.8 us
    psum x1, waiting for transfers between devices, per_device(): summed_mats, forward_feed = lax.psum((local_mats, local_feed), 'xr')  66.6 us
    psum x1, blocking collectives, per_device(): summed_mats, forward_feed = lax.psum((local_mats, local_feed), 'xr')  26.4 us
    psum x1, blocking collectives, per_device(): backward_feed = lax.psum(jnp.stack(back_list), 'xr')  25.4 us
    ppermute x4, starting transfers between devices, padded_2(): lax.ppermute(lax.slice_in_dim(block, 0, width, axis=dim), axis, backward)  11.2 us
    sub x1, other arithmetic, coupling_matrix(): inverse_pair[0] * cos_rows - inverse_pair[1] * sin_rows  9.44 us
  transfers between devices with their start and end apart: 11, of which 4 were waited for; matrix products, arithmetic and copies ran while one was open for 35% of the time, Pallas kernels for 0%

commit v1 on v0

v1 whole, which is shorter than its diff:
```python
import functools
import math

import jax
import jax.numpy as jnp
import numpy as np
from jax import lax
from jax.experimental import pallas as pl
from jax.experimental.pallas import tpu as pltpu
from jax.sharding import PartitionSpec as P

F = 2
Q = 64
H = 3
LMAX = 24
RD = 16
XD = 128
SIDE = 2 * H + 1
MESH = pl.DeviceIdType.MESH
f32 = jnp.float32
bf16 = jnp.bfloat16
i32 = jnp.int32


def phase_tables():
    turn = 2.0 * math.pi / 64
    power = np.arange(16) - 7
    cols = np.arange(XD)
    ang = turn * ((power[:, None] * cols[None, :]) % 64)
    v_rows = np.stack([np.cos(ang), np.sin(ang)]).astype(np.float32)
    u_rows = np.zeros((4, RD, 2, 16, XD), np.float32)
    cell = np.zeros((4, 12, RD, XD), np.float32)
    for dm in range(4):
        rows = 16 * dm + np.arange(RD)
        ang = turn * ((power[None, :] * rows[:, None]) % 64)
        u_rows[dm, :, 0] = np.cos(ang)[:, :, None]
        u_rows[dm, :, 1] = np.sin(ang)[:, :, None]
        for way, sign in enumerate((1, -1)):
            for f in range(F):
                ang = turn * ((sign * (1 + 2 * f) * rows[:, None] + (f - 4) * cols[None, :]) % 64)
                cell[dm, way * 4 + f * 2] = np.cos(ang)
                cell[dm, way * 4 + f * 2 + 1] = np.sin(ang)
        ang = turn * ((rows[:, None] + 0 * cols[None, :]) % 64)
        cell[dm, 8], cell[dm, 9] = np.cos(ang), np.sin(ang)
        ang = turn * ((0 * rows[:, None] + cols[None, :]) % 64)
        cell[dm, 10], cell[dm, 11] = np.cos(ang), np.sin(ang)
    return v_rows, u_rows, cell


def sincos_small(t):
    q = t * t
    s = t * (1.0 + q * (-1.0 / 6 + q * (1.0 / 120 + q * (-1.0 / 5040 + q * (1.0 / 362880)))))
    c = 1.0 + q * (-0.5 + q * (1.0 / 24 + q * (-1.0 / 720 + q * (1.0 / 40320))))
    return s, c


def sincos(t):
    q = t * t
    s = t * (
        1.0
        + q
        * (
            -1.0 / 6
            + q * (1.0 / 120 + q * (-1.0 / 5040 + q * (1.0 / 362880 + q * (-1.0 / 39916800))))
        )
    )
    c = 1.0 + q * (
        -0.5
        + q
        * (
            1.0 / 24
            + q
            * (-1.0 / 720 + q * (1.0 / 40320 + q * (-1.0 / 3628800 + q * (1.0 / 479001600))))
        )
    )
    return s, c


def squared(c, s):
    return c * c - s * s, 2.0 * (c * s)


def lanes_of(shape):
    return lax.broadcasted_iota(i32, shape, 1)


def rows_of(shape):
    return lax.broadcasted_iota(i32, shape, 0)


def pick(value, index):
    return jnp.take_along_axis(value, index, axis=1, mode="promise_in_bounds")


def split(value):
    high = value.astype(bf16)
    return high, (value - high.astype(f32)).astype(bf16)


def contract(left, right):
    return lax.dot_general(left, right, (((1,), (1,)), ((), ())), preferred_element_type=f32)


def contract3(left_high, left_low, right_high, right_low):
    return (
        contract(left_high, right_high)
        + contract(left_high, right_low)
        + contract(left_low, right_high)
    )


def regroup(value):
    shape = (8, 128)
    part = (rows_of(shape) - lanes_of(shape) // 16) & 7
    out = jnp.zeros(shape, f32)
    for s in range(8):
        moved = value
        if s:
            moved = pltpu.roll(pltpu.roll(value, 128 - 16 * s, 1), s, 0)
        out = jnp.where(part == s, moved, out)
    return out


def kernel(
    nd, nx,
    inc, zin, prev, hts, nbr, cnt, trn, aw, v_rows, u_hbm, cell_hbm,
    out_f, out_c,
    u_rows, cell, cbuf, edge_l, edge_r, pk_l, pk_r,
    cbuf2, edge_l2, edge_r2, pk_l2, pk_r2,
    shifted, table, tab_u_h, tab_u_l, tab_a_h, tab_a_l, tab_v, tab_f_h, tab_f_l,
    srcp, loaded, driven, weakf, w_lane, w_sub, row_buf,
    gx, gmsg, gr, fx, fx2, fmsg, fmsg2, fr, mats, state,
    base, vu,
    csem, hs_sem, hr_sem, hs2_sem, hr2_sem,
    gxs, gxr, grs, grr, fxs, fxr, fxs2, fxr2, frs, frr,
):
    d = lax.axis_index("rng")
    x = lax.axis_index("xr")
    dm = lax.rem(d, 4)
    spread = 1.0 / math.sqrt(RD * XD * nx)
    up, down = lax.rem(d + nd - 1, nd), lax.rem(d + 1, nd)
    left, right = lax.rem(x + nx - 1, nx), lax.rem(x + 1, nx)

    cu = pltpu.make_async_copy(u_hbm.at[dm], u_rows, csem.at[0])
    cc = pltpu.make_async_copy(cell_hbm.at[dm], cell, csem.at[1])
    cu.start()
    cc.start()

    barrier = pltpu.get_barrier_semaphore()

    def greet_rng(off, carry):
        pl.semaphore_signal(barrier, inc=1, device_id=(lax.rem(d + off, nd), x), device_id_type=MESH)
        return carry

    def greet_xr(off, carry):
        pl.semaphore_signal(barrier, inc=1, device_id=(d, lax.rem(x + off, nx)), device_id_type=MESH)
        return carry

    lax.fori_loop(1, nd, greet_rng, 0)
    lax.fori_loop(1, nx, greet_xr, 0)
    for dd in (up, down):
        for xx in (left, right):
            pl.semaphore_signal(barrier, inc=1, device_id=(dd, xx), device_id_type=MESH)

    wide = (RD, XD)
    lane16 = lanes_of(wide)
    small = (8, 128)
    lane8 = lanes_of(small)
    sub8 = rows_of(small)

    def pack_edges(parts, to_left, to_right):
        a = jnp.zeros(wide, f32)
        b = jnp.zeros(wide, f32)
        for c, part in enumerate(parts):
            here = lane16 // 8 == c
            a = jnp.where(here, part if c == 0 else pltpu.roll(part, 8 * c, 1), a)
            b = jnp.where(here, pltpu.roll(part, 8 * c + 3, 1), b)
        to_left[...] = a
        to_right[...] = b

    for c in range(4):
        cbuf[c, 8:24, :] = prev[c]
    cbuf[4, 8:24, :] = hts[...]
    pack_edges([prev[0], prev[1], prev[2], prev[3], hts[...]], pk_l, pk_r)
    zero8 = jnp.zeros(small, f32)
    for slot in (0, nd + 1):
        gr[slot] = zero8
        fr[slot] = zero8

    pl.semaphore_wait(barrier, nd - 1 + nx - 1 + 4)

    def halo(buf, e_l, e_r, p_l, p_r, send, recv):
        plan = [
            (buf.at[:, 8:16, :], buf.at[:, 24:32, :], (up, x)),
            (buf.at[:, 16:24, :], buf.at[:, 0:8, :], (down, x)),
            (p_l, e_r.at[8:24, :], (d, left)),
            (p_r, e_l.at[8:24, :], (d, right)),
            (p_l.at[0:8, :], e_r.at[24:32, :], (up, left)),
            (p_l.at[8:16, :], e_r.at[0:8, :], (down, left)),
            (p_r.at[0:8, :], e_l.at[24:32, :], (up, right)),
            (p_r.at[8:16, :], e_l.at[0:8, :], (down, right)),
        ]
        return [
            pltpu.make_async_remote_copy(
                src_ref=src, dst_ref=dst, send_sem=send.at[n], recv_sem=recv.at[n],
                device_id=dev, device_id_type=MESH,
            )
            for n, (src, dst, dev) in enumerate(plan)
        ]

    halo1 = halo(cbuf, edge_l, edge_r, pk_l, pk_r, hs_sem, hr_sem)
    for copy in halo1:
        copy.start()

    cu.wait()
    power16 = (rows_of(wide) - 7).astype(f32) * 0.03

    def fill(r, carry):
        at = pl.ds(pl.multiple_of(r * XD, XD), XD)
        hrow = jnp.broadcast_to(hts[pl.ds(r, 1), :], wide)
        hs, hc = sincos_small(power16 * hrow)
        vc0, vs0 = v_rows[0], v_rows[1]
        vc = hc * vc0 - hs * vs0
        vs = hc * vs0 + hs * vc0
        tab_v[0, :, at] = vc[:8]
        tab_v[1, :, at] = vs[:8]
        c8, s8 = squared(*squared(*squared(hc, hs)))
        pc, ps = u_rows[r, 0], u_rows[r, 1]
        cc_, ss_, cs_, sc_ = c8 * pc, s8 * ps, c8 * ps, s8 * pc
        for n, value in enumerate((cc_ - ss_, sc_ + cs_, cc_ + ss_, sc_ - cs_)):
            high, low = split(value)
            tab_u_h[16 * n : 16 * n + 16, at] = high
            tab_u_l[16 * n : 16 * n + 16, at] = low
        for f in range(F):
            zr = jnp.broadcast_to(zin[2 * f, pl.ds(r, 1), :], wide)
            zi = jnp.broadcast_to(zin[2 * f + 1, pl.ds(r, 1), :], wide)
            for n, value in enumerate((zr * vc - zi * vs, zr * vs + zi * vc)):
                high, low = split(value)
                k = 2 * f + n
                tab_a_h[16 * k : 16 * k + 16, at] = high
                tab_a_l[16 * k : 16 * k + 16, at] = low
        return carry

    lax.fori_loop(0, RD, fill, 0)

    y = contract3(tab_u_h[...], tab_u_l[...], tab_a_h[...], tab_a_l[...])
    yc = jnp.concatenate([y[0:16], y[32:48]], axis=1)
    ys = jnp.concatenate([y[16:32], y[48:64]], axis=1)
    gx[x] = yc + jnp.where((lane16 // 16) % 2 == 0, -pltpu.roll(ys, 112, 1), pltpu.roll(ys, 16, 1))

    def spread_xr(buf, send, recv):
        def step(off, carry):
            pltpu.make_async_remote_copy(
                src_ref=buf.at[x], dst_ref=buf.at[x], send_sem=send, recv_sem=recv,
                device_id=(d, lax.rem(x + off, nx)), device_id_type=MESH,
            ).start()
            return carry

        lax.fori_loop(1, nx, step, 0)

    def await_bytes(view, sem):
        pltpu.make_async_copy(view, view, sem).wait()

    def total_xr(buf):
        total = buf[0]
        for k in range(1, nx):
            total = total + buf[k]
        return total

    spread_xr(gx, gxs, gxr)

    row_buf[...] = zero8
    for f in range(F):
        for c in range(2):
            row_buf[2 * f + c : 2 * f + c + 1, 0:Q] = aw[f, c : c + 1, :]
    row_buf[4:6, 0:Q] = trn[0]
    li, lj = lane8 // 16, lane8 % 16
    lane_rows = jnp.where(lj < 8, pick(row_buf[...], (li * 8 + lj) & 127), 0.0)
    for k in range(4):
        row = jnp.broadcast_to(lane_rows[k : k + 1, :], small) * spread
        w_lane[k] = row
        for i in range(8):
            w_sub[k, i] = pick(row, sub8 + 16 * i)

    cc.wait()
    hh = hts[...]
    hs, hc = sincos_small(0.03 * hh)
    c8, s8 = squared(*squared(*squared(hc, hs)))
    vu[0] = hc * cell[10] - hs * cell[11]
    vu[1] = hc * cell[11] + hs * cell[10]
    vu[2] = c8 * cell[8] - s8 * cell[9]
    vu[3] = s8 * cell[8] + c8 * cell[9]
    vu[4] = c8 * cell[8] + s8 * cell[9]
    vu[5] = s8 * cell[8] - c8 * cell[9]
    for f in range(F):
        s, c = sincos((0.3 + 0.2 * f) * hh)
        for way in range(2):
            k = way * 4 + f * 2
            base[k] = c * cell[k] - s * cell[k + 1]
            base[k + 1] = s * cell[k] + c * cell[k + 1]

    def note(l, words):
        word0, word1 = words
        code = nbr[l]
        m = jnp.where(code >= 24, code + 1, code)
        low = m < 28
        bit = jnp.where(l < cnt[...], jnp.left_shift(1, jnp.where(low, m, m - 28)), 0)
        return word0 | jnp.where(low, bit, 0), word1 | jnp.where(low, 0, bit)

    zero_word = jnp.zeros(wide, i32)
    words = lax.fori_loop(0, LMAX, note, (zero_word, zero_word))

    tall = (32, XD)
    lane32 = lanes_of(tall)
    row32 = rows_of(tall) + (d * RD - 8)
    inside = (row32 >= 0) & (row32 < nd * RD)

    def shift_all(buf, e_l, e_r, count):
        el = jnp.where(inside & (lane32 < 128 * x), e_l[...], 0.0)
        er = jnp.where(inside & (lane32 < 128 * (nx - 1 - x)), e_r[...], 0.0)
        for c in range(count):
            mid = jnp.where(inside, buf[c], 0.0)
            shifted[H, c] = mid
            for k in range(1, H + 1):
                shifted[H + k, c] = jnp.where(
                    lane32 >= 128 - k,
                    pltpu.roll(er, (128 - k - 8 * c) % 128, 1),
                    pltpu.roll(mid, 128 - k, 1),
                )
                shifted[H - k, c] = jnp.where(
                    lane32 < k,
                    pltpu.roll(el, (k - 3 - 8 * c) % 128, 1),
                    pltpu.roll(mid, k, 1),
                )

    def window(dyi, c, dx):
        return shifted[dyi, c, 8 + dx : 24 + dx, :]

    def applied(total, g, dyi, dx):
        out = []
        for f in range(F):
            gr_, gi_ = g[2 * f], g[2 * f + 1]
            ur, ui = window(dyi, 2 * f, dx), window(dyi, 2 * f + 1, dx)
            out.append(total[2 * f] + (gr_ * ur - gi_ * ui))
            out.append(total[2 * f + 1] + (gr_ * ui + gi_ * ur))
        return tuple(out)

    for copy in halo1:
        copy.wait_recv()
    shift_all(cbuf, edge_l, edge_r, 5)

    def couple(dyi, total):
        dy = dyi - H
        for dxi in range(SIDE):
            dx = dxi - H
            square = jnp.maximum(dx * dx + dy * dy, 1).astype(f32)
            rise = window(dyi, 4, dx) - hh
            dist2 = square + rise * rise
            inv = lax.rsqrt(dist2)
            inv = inv * (1.5 - 0.5 * dist2 * (inv * inv))
            bits = words[dxi // 4] >> (7 * (dxi % 4) + dyi)
            mag = jnp.where((bits & 1) == 1, 0.25 * inv, 0.0)
            s1, c1 = sincos((math.pi / 8) * (dist2 * inv) - 0.5 * math.pi)
            s1, c1 = c1, -s1
            c4, s4 = squared(*squared(c1, s1))
            g = (
                mag * c4,
                mag * s4,
                mag * (c4 * c1 - s4 * s1),
                mag * (s4 * c1 + c4 * s1),
            )
            for c in range(4):
                table[dyi, dxi, c] = g[c]
            total = applied(total, g, dyi, dx)
        return total

    def recouple(dyi, total):
        for dxi in range(SIDE):
            g = [table[dyi, dxi, c] for c in range(4)]
            total = applied(total, g, dyi, dxi - H)
        return total

    nothing = (jnp.zeros(wide, f32),) * 4
    near_old = lax.fori_loop(0, SIDE, couple, nothing)

    def times_z(f, real, imag):
        zr, zi = zin[2 * f], zin[2 * f + 1]
        return zr * real - zi * imag, zr * imag + zi * real

    def project(way, field, buf, send, recv):
        for f in range(F):
            k = way * 4 + f * 2
            br, bi = base[k], base[k + 1]
            sr, si = field[2 * f], field[2 * f + 1]
            srcp[2 * f] = br * sr + bi * si
            srcp[2 * f + 1] = br * si - bi * sr

        def lay(r, carry):
            at = pl.ds(pl.multiple_of(r * XD, XD), XD)
            vc, vs = tab_v[0, :, at], tab_v[1, :, at]
            for f in range(F):
                sr = jnp.broadcast_to(srcp[2 * f, pl.ds(r, 1), :], small)
                si = jnp.broadcast_to(srcp[2 * f + 1, pl.ds(r, 1), :], small)
                both = jnp.concatenate([sr * vc - si * vs, sr * vs + si * vc], axis=0)
                high, low = split(both)
                tab_f_h[16 * f : 16 * f + 16, at] = high
                tab_f_l[16 * f : 16 * f + 16, at] = low
            return carry

        lax.fori_loop(0, RD, lay, 0)
        rows = slice(32 * way, 32 * way + 32)
        y = contract3(tab_u_h[rows, :], tab_u_l[rows, :], tab_f_h[...], tab_f_l[...])
        pad = jnp.zeros((8, 96), f32)
        yc = jnp.concatenate([y[0:8], pad], axis=1)
        ys = jnp.concatenate([y[16:24], pad], axis=1)
        buf[x] = yc + jnp.where((lane8 // 8) % 2 == 0, -pltpu.roll(ys, 120, 1), pltpu.roll(ys, 8, 1))
        spread_xr(buf, send, recv)

    for f in range(F):
        sr, si = times_z(f, inc[2 * f] - near_old[2 * f], inc[2 * f + 1] - near_old[2 * f + 1])
        loaded[2 * f] = sr
        loaded[2 * f + 1] = si
    project(0, loaded, fx, fxs, fxr)

    await_bytes(gx.at[pl.ds(0, nx - 1)], gxr)
    g_sum = total_xr(gx)
    h0, h1 = regroup(g_sum[:8]), regroup(g_sum[8:])
    gmsg[0] = jnp.where(sub8 < 4, h0, pltpu.roll(h1, 4, 0))
    gmsg[1] = jnp.where(sub8 < 4, pltpu.roll(h0, 4, 0), h1)

    def send_g(off, carry):
        pltpu.make_async_remote_copy(
            src_ref=gmsg.at[(d + off) // nd], dst_ref=gr.at[d + 1],
            send_sem=grs, recv_sem=grr.at[d],
            device_id=(lax.rem(d + off, nd), x), device_id_type=MESH,
        ).start()
        return carry

    lax.fori_loop(1, nd, send_g, 0)

    def send_feed(buf, recv, msg, first, last):
        await_bytes(buf.at[pl.ds(0, nx - 1)], recv)
        total = total_xr(buf)
        out = lane_rows
        for k in range(4):
            spreadout = pick(total, (8 * k + 7 - lj) & 127)
            spreadout = jnp.where((sub8 == 7 - li) & (lj < 8), spreadout, 0.0)
            row = jnp.sum(spreadout, axis=0, keepdims=True)
            out = jnp.where(sub8 == k, jnp.broadcast_to(row, small), out)
        msg[...] = out

        def step(to, carry):
            pltpu.make_async_remote_copy(
                src_ref=msg, dst_ref=fr.at[d + 1], send_sem=frs, recv_sem=frr.at[d],
                device_id=(to, x), device_id_type=MESH,
            ).start()
            return carry

        lax.fori_loop(first, last, step, 0)

    def await_slots(buf, sem, first, last):
        def step(k, carry):
            await_bytes(buf.at[k + 1], sem.at[k])
            return carry

        lax.fori_loop(first, last, step, 0)

    def build(slot, first):
        if first:
            start = (7 - li) * 16 + sub8 - lj + 7
        else:
            start = (li + 7) * 16 + lj - sub8 + 7
        for f in range(F):
            half = [
                [jnp.broadcast_to(gr[slot, r : r + 1, :], small) for r in (2 * f + c, 4 + 2 * f + c)]
                for c in range(2)
            ]
            for i in range(8):
                src = start + 16 * i if first else start - 16 * i
                index = src & 127
                near = src < 128
                mr = jnp.where(near, pick(half[0][0], index), pick(half[0][1], index))
                mi = jnp.where(near, pick(half[1][0], index), pick(half[1][1], index))
                own = lane8 == sub8 + 16 * i
                if first:
                    wr, wi = w_sub[2 * f, i], w_sub[2 * f + 1, i]
                else:
                    wr, wi = w_lane[2 * f], w_lane[2 * f + 1]
                    own = own | (lane8 == sub8 + (16 * i + 8))
                mats[slot, f, 0, i] = jnp.where(own, 1.0, 0.0) - (mr * wr - mi * wi)
                mats[slot, f, 1, i] = -(mr * wi + mi * wr)

    def slots_of(way, t):
        if way == 0:
            at = 2 * t - lax.rem(d, 2)
            return at + 1, at + 2
        at = 2 * t - lax.rem(nd - 1 - d, 2)
        return nd - at, nd - at - 1

    def pairs_of(way):
        return (d + 1) // 2 if way == 0 else (nd - d) // 2

    def build_all(way):
        if way == 0:
            await_slots(gr, grr, 0, d)
        else:
            await_slots(gr, grr, d + 1, nd)

        def step(t, carry):
            one, two = slots_of(way, t)
            build(one, True)
            build(two, False)
            return carry

        lax.fori_loop(0, pairs_of(way), step, 0)

    def sweep(way):
        if way == 0:
            await_slots(fr, frr, 0, d)
        else:
            await_slots(fr, frr, d + 1, nd)
        for f in range(F):
            for c in range(2):
                for i in range(8):
                    state[f, c, i] = zero8

        def row(slot, k):
            return jnp.broadcast_to(fr[slot, k : k + 1, :], small)

        def step(t, carry):
            one, two = slots_of(way, t)
            for f in range(F):
                ar = ai = zero8
                for i in range(8):
                    mr, mi = mats[one, f, 0, i], mats[one, f, 1, i]
                    sr, si = state[f, 0, i], state[f, 1, i]
                    ar = ar + (mr * sr - mi * si)
                    ai = ai + (mr * si + mi * sr)
                share = row(one, 4 + f)
                yr = share * (jnp.sum(ar, axis=0, keepdims=True) + row(one, 2 * f))
                yi = share * (jnp.sum(ai, axis=0, keepdims=True) + row(one, 2 * f + 1))
                yr = yr + pltpu.roll(row(two, 2 * f), 8, 1)
                yi = yi + pltpu.roll(row(two, 2 * f + 1), 8, 1)
                share = row(two, 4 + f)
                for i in range(8):
                    mr, mi = mats[two, f, 0, i], mats[two, f, 1, i]
                    own = pick(share, sub8 + 16 * i)
                    vr = jnp.sum(mr * yr - mi * yi, axis=1, keepdims=True)
                    vi = jnp.sum(mr * yi + mi * yr, axis=1, keepdims=True)
                    state[f, 0, i] = own * vr
                    state[f, 1, i] = own * vi
            return carry

        lax.fori_loop(0, pairs_of(way), step, 0)

    def radiate(way):
        for f in range(F):
            for i in range(8):
                wr, wi = w_sub[2 * f, i], w_sub[2 * f + 1, i]
                sr, si = state[f, 0, i], state[f, 1, i]
                state[f, 0, i] = wr * sr - wi * si
                state[f, 1, i] = wr * si + wi * sr
        vr, vi = vu[0], vu[1]
        ur, ui = vu[2 + 2 * way], vu[3 + 2 * way]

        def step(n, total):
            i = 7 - n
            out = []
            for f in range(F):
                tr, ti = total[2 * f], total[2 * f + 1]

                def coef(c, j):
                    return jnp.broadcast_to(state[f, c, i, j : j + 1, :], wide)

                ar, ai = coef(0, 7), coef(1, 7)
                for j in range(6, -1, -1):
                    ar, ai = ar * vr - ai * vi + coef(0, j), ar * vi + ai * vr + coef(1, j)
                out += [tr * ur - ti * ui + ar, tr * ui + ti * ur + ai]
            return tuple(out)

        total = lax.fori_loop(0, 8, step, nothing)
        out = []
        for f in range(F):
            k = way * 4 + f * 2
            br, bi = base[k], base[k + 1]
            tr, ti = total[2 * f], total[2 * f + 1]
            out += [br * tr - bi * ti, br * ti + bi * tr]
        return out

    send_feed(fx, fxr, fmsg, d + 1, nd)
    build_all(0)
    sweep(0)
    weak = radiate(0)
    flow = []
    for f in range(F):
        ar, ai = times_z(f, weak[2 * f], weak[2 * f + 1])
        flow += [loaded[2 * f] - ar, loaded[2 * f + 1] - ai]
    for c in range(4):
        out_f[c] = flow[c]
        cbuf2[c, 8:24, :] = flow[c]
        weakf[c] = weak[c]
    pack_edges(flow, pk_l2, pk_r2)
    halo2 = halo(cbuf2, edge_l2, edge_r2, pk_l2, pk_r2, hs2_sem, hr2_sem)
    for copy in halo2:
        copy.start()

    build_all(1)
    for copy in halo2:
        copy.wait_recv()
    shift_all(cbuf2, edge_l2, edge_r2, 4)
    near_new = lax.fori_loop(0, SIDE, recouple, nothing)
    for f in range(F):
        dr, di = times_z(
            f,
            inc[2 * f] - near_new[2 * f] - weakf[2 * f],
            inc[2 * f + 1] - near_new[2 * f + 1] - weakf[2 * f + 1],
        )
        driven[2 * f] = dr
        driven[2 * f + 1] = di
    project(1, driven, fx2, fxs2, fxr2)
    send_feed(fx2, fxr2, fmsg2, 0, d)
    sweep(1)
    weak = radiate(1)
    for f in range(F):
        ar, ai = times_z(f, weak[2 * f], weak[2 * f + 1])
        out_c[2 * f] = driven[2 * f] - ar
        out_c[2 * f + 1] = driven[2 * f + 1] - ai

    for copy in halo1 + halo2:
        copy.wait_send()
    await_bytes(gx.at[pl.ds(0, nx - 1)], gxs)
    await_bytes(fx.at[pl.ds(0, nx - 1)], fxs)
    await_bytes(fx2.at[pl.ds(0, nx - 1)], fxs2)
    await_bytes(gr.at[pl.ds(0, nd - 1)], grs)
    await_bytes(fr.at[pl.ds(0, nd - 1)], frs)


def solution(mesh):
    nd, nx = mesh.shape["rng"], mesh.shape["xr"]
    v_rows, u_rows, cell = phase_tables()

    def per_device(incident, inverse_diag, previous, heights, neighbours, counts, transmit, angle_weights):
        vmem = pl.BlockSpec(memory_space=pltpu.VMEM)
        anywhere = pl.BlockSpec(memory_space=pl.ANY)
        points = RD * XD
        block = jax.ShapeDtypeStruct((2 * F, RD, XD), f32)
        V = pltpu.VMEM
        dma = pltpu.SemaphoreType.DMA
        scratch = [
            V((RD, 2, 16, XD), f32), V((12, RD, XD), f32),
            V((5, 32, XD), f32), V((32, XD), f32), V((32, XD), f32), V((RD, XD), f32), V((RD, XD), f32),
            V((4, 32, XD), f32), V((32, XD), f32), V((32, XD), f32), V((RD, XD), f32), V((RD, XD), f32),
            V((SIDE, 5, 32, XD), f32), V((SIDE, SIDE, 4, RD, XD), f32),
            V((64, points), bf16), V((64, points), bf16), V((64, points), bf16), V((64, points), bf16),
            V((2, 8, points), f32), V((32, points), bf16), V((32, points), bf16),
            V((4, RD, XD), f32), V((4, RD, XD), f32), V((4, RD, XD), f32), V((4, RD, XD), f32),
            V((4, 8, 128), f32), V((4, 8, 8, 128), f32), V((8, 128), f32),
            V((nx, 16, 128), f32), V((2, 8, 128), f32), V((nd + 2, 8, 128), f32),
            V((nx, 8, 128), f32), V((nx, 8, 128), f32), V((8, 128), f32), V((8, 128), f32),
            V((nd + 2, 8, 128), f32), V((nd + 2, F, 2, 8, 8, 128), f32), V((F, 2, 8, 8, 128), f32),
            V((8, RD, XD), f32), V((6, RD, XD), f32),
            dma((2,)), dma((8,)), dma((8,)), dma((8,)), dma((8,)),
            dma, dma, dma, dma((nd,)), dma, dma, dma, dma, dma, dma((nd,)),
        ]
        return pl.pallas_call(
            functools.partial(kernel, nd, nx),
            out_shape=(block, block),
            in_specs=[vmem] * 9 + [anywhere] * 2,
            out_specs=(vmem, vmem),
            scratch_shapes=scratch,
            compiler_params=pltpu.CompilerParams(
                collective_id=0, has_side_effects=True, vmem_limit_bytes=40 << 20
            ),
        )(
            incident, inverse_diag, previous, heights, neighbours, counts, transmit, angle_weights,
            jnp.asarray(v_rows), jnp.asarray(u_rows), jnp.asarray(cell),
        )

    placed = (
        P(None, "rng", "xr"),
        P(None, "rng", "xr"),
        P(None, "rng", "xr"),
        P("rng", "xr"),
        P(None, "rng", "xr"),
        P("rng", "xr"),
        P("rng", None, None),
        P(),
    )
    return jax.shard_map(
        per_device,
        mesh=mesh,
        in_specs=placed,
        out_specs=(P(None, "rng", "xr"), P(None, "rng", "xr")),
        check_vma=False,
    )
```

time: 460 us -> 74.6 us (0.16)
  the two profiles are of different devices: /device:TPU:8 before, /device:TPU:1 now
where the time goes in v1:
time: 74.6 us; the launch traced here: 74 us
  Pallas kernels  63.2 us (85%)
  local copies, waits for them, and re-layouts  10.1 us (14%)
    pallas_call x1, Pallas kernels, per_device(): pl.pallas_call(functools.partial(kernel, nd, nx), out_shape=(block, block...  63.2 us
    unnamed x24, local copies, waits for them, and re-layouts  10.1 us

profile of v1, /device:TPU:1, one launch (start us, length us, event | category | flops | bytes accessed | tf_op | source)
XLA Modules:
  0.0 74.0 jit_solution(9025859402166989344)
XLA Ops:
  0.6 0.0 copy-start
  0.6 1.2 %copy-done = f32[4,16,2,16,128]{4,3,2,1,0:T(8,128)S(1)} copy-done((f32[4,16,2,16,128]{4,3,2,1,0:T(8,128)S(1)}, f32[4,16,2,16,128]{4,3,2,1,0:T(8,128)}, u32[]{:S(2)}) %copy-start) | copy-done | bytes 1048600
  1.9 0.0 copy-start.1
  1.9 1.0 %copy-done.1 = f32[4,12,16,128]{3,2,1,0:T(8,128)S(1)} copy-done((f32[4,12,16,128]{3,2,1,0:T(8,128)S(1)}, f32[4,12,16,128]{3,2,1,0:T(8,128)}, u32[]{:S(2)}) %copy-start.1) | copy-done | bytes 393240
  2.9 0.0 copy-start.2
  2.9 0.9 %copy-done.2 = s32[24,16,128]{2,1,0:T(8,128)S(1)} copy-done((s32[24,16,128]{2,1,0:T(8,128)S(1)}, s32[24,16,128]{2,1,0:T(8,128)}, u32[]{:S(2)}) %copy-start.2) | copy-done | bytes 196632
  3.8 0.0 copy-start.3
  3.8 0.8 %copy-done.3 = f32[4,16,128]{2,1,0:T(8,128)S(1)} copy-done((f32[4,16,128]{2,1,0:T(8,128)S(1)}, f32[4,16,128]{2,1,0:T(8,128)}, u32[]{:S(2)}) %copy-start.3) | copy-done | bytes 32792
  4.5 0.0 copy-start.4
  4.5 0.8 %copy-done.4 = f32[4,16,128]{2,1,0:T(8,128)S(1)} copy-done((f32[4,16,128]{2,1,0:T(8,128)S(1)}, f32[4,16,128]{2,1,0:T(8,128)}, u32[]{:S(2)}) %copy-start.4) | copy-done | bytes 32792
  5.3 0.0 copy-start.5
  5.3 0.8 %copy-done.5 = f32[4,16,128]{2,1,0:T(8,128)S(1)} copy-done((f32[4,16,128]{2,1,0:T(8,128)S(1)}, f32[4,16,128]{2,1,0:T(8,128)}, u32[]{:S(2)}) %copy-start.5) | copy-done | bytes 32792
  6.1 0.0 copy-start.6
  6.1 0.7 copy-done.6
  6.8 0.0 copy-start.7
  6.8 0.7 copy-done.7
  7.5 0.0 copy-start.8
  7.5 0.7 copy-done.8
  8.2 0.0 copy-start.9
  8.2 0.7 copy-done.9
  8.9 0.0 copy-start.10
  8.9 0.7 copy-done.10
  9.5 63.2 %shard_map.122 = (f32[4,16,128]{2,1,0:T(8,128)S(1)}, f32[4,16,128]{2,1,0:T(8,128)S(1)}) custom-call(f32[4,16,128]{2,1,0:T(8,128)S(1)} %copy-done.3, f32[4,16,128]{2,1,0:T(8,128)S(1)} %copy-done.4, f32[4,16,128]{2,1,0:T(8,128)S(1)} %copy-done.5, f32[16,128]{1,0:T(8,128)S(1)} %copy-done.7, s32[24,16,128]{2,1,0:T(8,128)S(1)} %copy-done.2, ...), custom_call_target="tpu_custom_call" | custom-call | tf_op jit(solution)/shard_map/pallas_call | solution.py:665
  72.7 0.6 copy.15
  73.3 0.6 copy.16
Async XLA Ops:
  0.6 1.2 %copy-start = (f32[4,16,2,16,128]{4,3,2,1,0:T(8,128)S(1)}, f32[4,16,2,16,128]{4,3,2,1,0:T(8,128)}, u32[]{:S(2)}) copy-start(f32[4,16,2,16,128]{4,3,2,1,0:T(8,128)} %constant.7.clone.u_hbm) | copy-start | bytes 3145732
  1.9 1.0 %copy-start.1 = (f32[4,12,16,128]{3,2,1,0:T(8,128)S(1)}, f32[4,12,16,128]{3,2,1,0:T(8,128)}, u32[]{:S(2)}) copy-start(f32[4,12,16,128]{3,2,1,0:T(8,128)} %constant.8.clone.cell_hbm) | copy-start | bytes 1179652
  2.9 0.9 %copy-start.2 = (s32[24,16,128]{2,1,0:T(8,128)S(1)}, s32[24,16,128]{2,1,0:T(8,128)}, u32[]{:S(2)}) copy-start(s32[24,16,128]{2,1,0:T(8,128)} %nbr.1) | copy-start | bytes 589828
  3.8 0.8 %copy-start.3 = (f32[4,16,128]{2,1,0:T(8,128)S(1)}, f32[4,16,128]{2,1,0:T(8,128)}, u32[]{:S(2)}) copy-start(f32[4,16,128]{2,1,0:T(8,128)} %inc.1) | copy-start | bytes 98308
  4.5 0.8 %copy-start.4 = (f32[4,16,128]{2,1,0:T(8,128)S(1)}, f32[4,16,128]{2,1,0:T(8,128)}, u32[]{:S(2)}) copy-start(f32[4,16,128]{2,1,0:T(8,128)} %zin.1) | copy-start | bytes 98308
  5.3 0.8 %copy-start.5 = (f32[4,16,128]{2,1,0:T(8,128)S(1)}, f32[4,16,128]{2,1,0:T(8,128)}, u32[]{:S(2)}) copy-start(f32[4,16,128]{2,1,0:T(8,128)} %prev.1) | copy-start | bytes 98308
  6.1 0.7 copy-start.6
  6.8 0.7 copy-start.7
  7.5 0.7 copy-start.8
  8.2 0.7 copy-start.9
  8.9 0.7 copy-start.10

commit v2 on v1

--- a/solution.py
+++ b/solution.py
@@ -123,16 +123,16 @@
 
 def kernel(
     nd, nx,
-    inc, zin, prev, hts, nbr, cnt, trn, aw, v_rows, u_hbm, cell_hbm,
+    inc_hbm, zin_hbm, prev_hbm, hts_hbm, nbr_hbm, cnt_hbm, trn_hbm, aw_hbm, v_hbm, u_hbm, cell_hbm,
     out_f, out_c,
-    u_rows, cell, cbuf, edge_l, edge_r, pk_l, pk_r,
+    inc, zin, prev, hts, nbr, cnt, trn, aw, v_rows, u_rows, cell, cbuf, edge_l, edge_r, pk_l, pk_r,
     cbuf2, edge_l2, edge_r2, pk_l2, pk_r2,
     shifted, table, tab_u_h, tab_u_l, tab_a_h, tab_a_l, tab_v, tab_f_h, tab_f_l,
-    srcp, loaded, driven, weakf, w_lane, w_sub, row_buf,
+    srcp, loaded, driven, weakf, w_lane, w_sub, row_buf, share_msg, tr,
     gx, gmsg, gr, fx, fx2, fmsg, fmsg2, fr, mats, state,
     base, vu,
     csem, hs_sem, hr_sem, hs2_sem, hr2_sem,
-    gxs, gxr, grs, grr, fxs, fxr, fxs2, fxr2, frs, frr,
+    gxs, gxr, grs, grr, fxs, fxr, fxs2, fxr2, frs, frr, trs, trr,
 ):
     d = lax.axis_index("rng")
     x = lax.axis_index("xr")
@@ -141,26 +141,34 @@
     up, down = lax.rem(d + nd - 1, nd), lax.rem(d + 1, nd)
     left, right = lax.rem(x + nx - 1, nx), lax.rem(x + 1, nx)
 
-    cu = pltpu.make_async_copy(u_hbm.at[dm], u_rows, csem.at[0])
-    cc = pltpu.make_async_copy(cell_hbm.at[dm], cell, csem.at[1])
-    cu.start()
-    cc.start()
+    def turned(value, by, size):
+        moved = value + by
+        return jnp.where(moved >= size, moved - size, moved)
+
+    nc = min(4, nd)
+    nr = nd // nc
+    far = lambda n, size: min(n, size - n)
+    others = sorted(
+        ((a, b) for a in range(nr) for b in range(nc) if a or b),
+        key=lambda p: -far(p[0], nr) - far(p[1], nc),
+    )
+    d_row, d_col = d // nc, lax.rem(d, nc)
+    blocks = [turned(d_row, a, nr) * nc + turned(d_col, b, nc) for a, b in others]
+    owners = [turned(x, n, nx) for n in sorted(range(1, nx), key=lambda n: -far(n, nx))]
 
     barrier = pltpu.get_barrier_semaphore()
-
-    def greet_rng(off, carry):
-        pl.semaphore_signal(barrier, inc=1, device_id=(lax.rem(d + off, nd), x), device_id_type=MESH)
-        return carry
-
-    def greet_xr(off, carry):
-        pl.semaphore_signal(barrier, inc=1, device_id=(d, lax.rem(x + off, nx)), device_id_type=MESH)
-        return carry
-
-    lax.fori_loop(1, nd, greet_rng, 0)
-    lax.fori_loop(1, nx, greet_xr, 0)
-    for dd in (up, down):
-        for xx in (left, right):
-            pl.semaphore_signal(barrier, inc=1, device_id=(dd, xx), device_id_type=MESH)
+    peers = [(to, x) for to in blocks] + [(d, to) for to in owners]
+    peers += [(dd, xx) for dd in (up, down) for xx in (left, right)]
+    for peer in peers:
+        pl.semaphore_signal(barrier, inc=1, device_id=peer, device_id_type=MESH)
+
+    fetches = [
+        (prev_hbm, prev), (hts_hbm, hts), (trn_hbm, trn), (v_hbm, v_rows), (u_hbm.at[dm], u_rows), (zin_hbm, zin),
+        (aw_hbm, aw), (cell_hbm.at[dm], cell), (cnt_hbm, cnt), (nbr_hbm, nbr), (inc_hbm, inc),
+    ]
+    fetches = [pltpu.make_async_copy(a, b, csem.at[n]) for n, (a, b) in enumerate(fetches)]
+    for fetch in fetches:
+        fetch.start()
 
     wide = (RD, XD)
     lane16 = lanes_of(wide)
@@ -178,27 +186,36 @@
         to_left[...] = a
         to_right[...] = b
 
+    for fetch in fetches[:2]:
+        fetch.wait()
     for c in range(4):
         cbuf[c, 8:24, :] = prev[c]
     cbuf[4, 8:24, :] = hts[...]
     pack_edges([prev[0], prev[1], prev[2], prev[3], hts[...]], pk_l, pk_r)
     zero8 = jnp.zeros(small, f32)
+    li, lj = lane8 // 16, lane8 % 16
     for slot in (0, nd + 1):
         gr[slot] = zero8
-        fr[slot] = zero8
+        fr[slot] = jnp.zeros((4, 128), f32)
+        tr[slot] = jnp.zeros((2, 128), f32)
+    fetches[2].wait()
+    row_buf[...] = zero8
+    row_buf[4:6, 0:Q] = trn[0]
+    share_rows = jnp.where(lj < 8, pick(row_buf[...], (li * 8 + lj) & 127), 0.0)
+    share_msg[...] = share_rows[4:6, :]
 
     pl.semaphore_wait(barrier, nd - 1 + nx - 1 + 4)
 
     def halo(buf, e_l, e_r, p_l, p_r, send, recv):
         plan = [
+            (p_l.at[0:8, :], e_r.at[24:32, :], (up, left)),
+            (p_l.at[8:16, :], e_r.at[0:8, :], (down, left)),
+            (p_r.at[0:8, :], e_l.at[24:32, :], (up, right)),
+            (p_r.at[8:16, :], e_l.at[0:8, :], (down, right)),
             (buf.at[:, 8:16, :], buf.at[:, 24:32, :], (up, x)),
             (buf.at[:, 16:24, :], buf.at[:, 0:8, :], (down, x)),
             (p_l, e_r.at[8:24, :], (d, left)),
             (p_r, e_l.at[8:24, :], (d, right)),
-            (p_l.at[0:8, :], e_r.at[24:32, :], (up, left)),
-            (p_l.at[8:16, :], e_r.at[0:8, :], (down, left)),
-            (p_r.at[0:8, :], e_l.at[24:32, :], (up, right)),
-            (p_r.at[8:16, :], e_l.at[0:8, :], (down, right)),
         ]
         return [
             pltpu.make_async_remote_copy(
@@ -211,8 +228,14 @@
     halo1 = halo(cbuf, edge_l, edge_r, pk_l, pk_r, hs_sem, hr_sem)
     for copy in halo1:
         copy.start()
-
-    cu.wait()
+    for to in blocks:
+        pltpu.make_async_remote_copy(
+            src_ref=share_msg, dst_ref=tr.at[d + 1], send_sem=trs, recv_sem=trr,
+            device_id=(to, x), device_id_type=MESH,
+        ).start()
+
+    for fetch in fetches[3:6]:
+        fetch.wait()
     power16 = (rows_of(wide) - 7).astype(f32) * 0.03
 
     def fill(r, carry):
@@ -249,14 +272,11 @@
     gx[x] = yc + jnp.where((lane16 // 16) % 2 == 0, -pltpu.roll(ys, 112, 1), pltpu.roll(ys, 16, 1))
 
     def spread_xr(buf, send, recv):
-        def step(off, carry):
+        for to in owners:
             pltpu.make_async_remote_copy(
                 src_ref=buf.at[x], dst_ref=buf.at[x], send_sem=send, recv_sem=recv,
-                device_id=(d, lax.rem(x + off, nx)), device_id_type=MESH,
+                device_id=(d, to), device_id_type=MESH,
             ).start()
-            return carry
-
-        lax.fori_loop(1, nx, step, 0)
 
     def await_bytes(view, sem):
         pltpu.make_async_copy(view, view, sem).wait()
@@ -269,20 +289,18 @@
 
     spread_xr(gx, gxs, gxr)
 
-    row_buf[...] = zero8
+    for fetch in fetches[6:]:
+        fetch.wait()
     for f in range(F):
         for c in range(2):
             row_buf[2 * f + c : 2 * f + c + 1, 0:Q] = aw[f, c : c + 1, :]
-    row_buf[4:6, 0:Q] = trn[0]
-    li, lj = lane8 // 16, lane8 % 16
-    lane_rows = jnp.where(lj < 8, pick(row_buf[...], (li * 8 + lj) & 127), 0.0)
+    weight_rows = [jnp.broadcast_to(row_buf[k : k + 1, :], small) * spread for k in range(4)]
     for k in range(4):
-        row = jnp.broadcast_to(lane_rows[k : k + 1, :], small) * spread
-        w_lane[k] = row
-        for i in range(8):
-            w_sub[k, i] = pick(row, sub8 + 16 * i)
-
-    cc.wait()
+        w_lane[k] = jnp.where(lj < 8, pick(weight_rows[k], (li * 8 + lj) & 127), 0.0)
+    for i in range(8):
+        for k in range(4):
+            w_sub[k, i] = pick(weight_rows[k], sub8 + 8 * i)
+
     hh = hts[...]
     hs, hc = sincos_small(0.03 * hh)
     c8, s8 = squared(*squared(*squared(hc, hs)))
@@ -388,6 +406,7 @@
         return zr * real - zi * imag, zr * imag + zi * real
 
     def project(way, field, buf, send, recv):
+        lj_even = (lane8 // 8) % 2 == 0
         for f in range(F):
             k = way * 4 + f * 2
             br, bi = base[k], base[k + 1]
@@ -413,7 +432,11 @@
         pad = jnp.zeros((8, 96), f32)
         yc = jnp.concatenate([y[0:8], pad], axis=1)
         ys = jnp.concatenate([y[16:24], pad], axis=1)
-        buf[x] = yc + jnp.where((lane8 // 8) % 2 == 0, -pltpu.roll(ys, 120, 1), pltpu.roll(ys, 8, 1))
+        sums = yc + jnp.where(lj_even, -pltpu.roll(ys, 120, 1), pltpu.roll(ys, 8, 1))
+        for k in range(4):
+            row = pick(sums, 8 * k + 7 - (lj & 7))
+            row = jnp.where(sub8 == 7 - li, row, 0.0)
+            buf[x, k : k + 1, :] = jnp.sum(row, axis=0, keepdims=True)
         spread_xr(buf, send, recv)
 
     for f in range(F):
@@ -428,35 +451,24 @@
     gmsg[0] = jnp.where(sub8 < 4, h0, pltpu.roll(h1, 4, 0))
     gmsg[1] = jnp.where(sub8 < 4, pltpu.roll(h0, 4, 0), h1)
 
-    def send_g(off, carry):
+    for to in blocks:
         pltpu.make_async_remote_copy(
-            src_ref=gmsg.at[(d + off) // nd], dst_ref=gr.at[d + 1],
+            src_ref=gmsg.at[(to < d).astype(i32)], dst_ref=gr.at[d + 1],
             send_sem=grs, recv_sem=grr.at[d],
-            device_id=(lax.rem(d + off, nd), x), device_id_type=MESH,
+            device_id=(to, x), device_id_type=MESH,
         ).start()
-        return carry
-
-    lax.fori_loop(1, nd, send_g, 0)
-
-    def send_feed(buf, recv, msg, first, last):
+
+    def send_feed(way, buf, recv, msg):
         await_bytes(buf.at[pl.ds(0, nx - 1)], recv)
-        total = total_xr(buf)
-        out = lane_rows
-        for k in range(4):
-            spreadout = pick(total, (8 * k + 7 - lj) & 127)
-            spreadout = jnp.where((sub8 == 7 - li) & (lj < 8), spreadout, 0.0)
-            row = jnp.sum(spreadout, axis=0, keepdims=True)
-            out = jnp.where(sub8 == k, jnp.broadcast_to(row, small), out)
-        msg[...] = out
-
-        def step(to, carry):
-            pltpu.make_async_remote_copy(
-                src_ref=msg, dst_ref=fr.at[d + 1], send_sem=frs, recv_sem=frr.at[d],
-                device_id=(to, x), device_id_type=MESH,
-            ).start()
-            return carry
-
-        lax.fori_loop(first, last, step, 0)
+        msg[...] = total_xr(buf)
+        for to in blocks:
+
+            @pl.when(to < d if way else to > d)
+            def _():
+                pltpu.make_async_remote_copy(
+                    src_ref=msg, dst_ref=fr.at[d + 1], send_sem=frs, recv_sem=frr.at[d],
+                    device_id=(to, x), device_id_type=MESH,
+                ).start()
 
     def await_slots(buf, sem, first, last):
         def step(k, carry):
@@ -470,25 +482,36 @@
             start = (7 - li) * 16 + sub8 - lj + 7
         else:
             start = (li + 7) * 16 + lj - sub8 + 7
-        for f in range(F):
-            half = [
-                [jnp.broadcast_to(gr[slot, r : r + 1, :], small) for r in (2 * f + c, 4 + 2 * f + c)]
-                for c in range(2)
-            ]
-            for i in range(8):
-                src = start + 16 * i if first else start - 16 * i
-                index = src & 127
-                near = src < 128
-                mr = jnp.where(near, pick(half[0][0], index), pick(half[0][1], index))
-                mi = jnp.where(near, pick(half[1][0], index), pick(half[1][1], index))
-                own = lane8 == sub8 + 16 * i
+        g = [
+            [jnp.broadcast_to(gr[slot, r : r + 1, :], small) for r in (k, 4 + k)]
+            for k in range(4)
+        ]
+        if not first:
+            index = (lane8 & 7) * 16 + sub8
+            shares = [pick(jnp.broadcast_to(tr[slot, f : f + 1, :], small), index) for f in range(F)]
+            shares = jnp.where(lane8 < 8, shares[0], shares[1])
+        for i in range(8):
+            src = start + 16 * i if first else start - 16 * i
+            index = src & 127
+            near = src < 128
+            m = [jnp.where(near, pick(g[k][0], index), pick(g[k][1], index)) for k in range(4)]
+            own = lane8 == sub8 + 16 * i
+            if not first:
+                own = own | (lane8 == sub8 + (16 * i + 8))
+            for f in range(F):
+                mr, mi = m[2 * f], m[2 * f + 1]
                 if first:
                     wr, wi = w_sub[2 * f, i], w_sub[2 * f + 1, i]
                 else:
                     wr, wi = w_lane[2 * f], w_lane[2 * f + 1]
-                    own = own | (lane8 == sub8 + (16 * i + 8))
-                mats[slot, f, 0, i] = jnp.where(own, 1.0, 0.0) - (mr * wr - mi * wi)
-                mats[slot, f, 1, i] = -(mr * wi + mi * wr)
+                real = jnp.where(own, 1.0, 0.0) - (mr * wr - mi * wi)
+                imag = -(mr * wi + mi * wr)
+                if not first:
+                    at = 8 * f + i
+                    share = jnp.broadcast_to(shares[:, at : at + 1], small)
+                    real, imag = share * real, share * imag
+                mats[slot, f, 0, i] = real
+                mats[slot, f, 1, i] = imag
 
     def slots_of(way, t):
         if way == 0:
@@ -500,12 +523,13 @@
     def pairs_of(way):
         return (d + 1) // 2 if way == 0 else (nd - d) // 2
 
+    def await_blocks(way, buf, sem):
+        if way == 0:
+            await_slots(buf, sem, 0, d)
+        else:
+            await_slots(buf, sem, d + 1, nd)
+
     def build_all(way):
-        if way == 0:
-            await_slots(gr, grr, 0, d)
-        else:
-            await_slots(gr, grr, d + 1, nd)
-
         def step(t, carry):
             one, two = slots_of(way, t)
             build(one, True)
@@ -515,40 +539,39 @@
         lax.fori_loop(0, pairs_of(way), step, 0)
 
     def sweep(way):
-        if way == 0:
-            await_slots(fr, frr, 0, d)
-        else:
-            await_slots(fr, frr, d + 1, nd)
         for f in range(F):
             for c in range(2):
                 for i in range(8):
                     state[f, c, i] = zero8
 
-        def row(slot, k):
-            return jnp.broadcast_to(fr[slot, k : k + 1, :], small)
+        def tree(terms):
+            while len(terms) > 1:
+                terms = [a + b for a, b in zip(terms[::2], terms[1::2])]
+            return terms[0]
 
         def step(t, carry):
             one, two = slots_of(way, t)
             for f in range(F):
-                ar = ai = zero8
+                tr_, ti_ = [], []
                 for i in range(8):
                     mr, mi = mats[one, f, 0, i], mats[one, f, 1, i]
                     sr, si = state[f, 0, i], state[f, 1, i]
-                    ar = ar + (mr * sr - mi * si)
-                    ai = ai + (mr * si + mi * sr)
-                share = row(one, 4 + f)
-                yr = share * (jnp.sum(ar, axis=0, keepdims=True) + row(one, 2 * f))
-                yi = share * (jnp.sum(ai, axis=0, keepdims=True) + row(one, 2 * f + 1))
-                yr = yr + pltpu.roll(row(two, 2 * f), 8, 1)
-                yi = yi + pltpu.roll(row(two, 2 * f + 1), 8, 1)
-                share = row(two, 4 + f)
+                    tr_.append(mr * sr - mi * si)
+                    ti_.append(mr * si + mi * sr)
+                share = tr[one, f : f + 1, :]
+                y = []
+                for c, terms in enumerate((tr_, ti_)):
+                    k = 2 * f + c
+                    row = share * (jnp.sum(tree(terms), axis=0, keepdims=True) + fr[one, k : k + 1, :])
+                    row = row + jnp.where(lj[:1] < 8, 0.0, fr[two, k : k + 1, :])
+                    y.append(jnp.broadcast_to(row, small))
+                yr, yi = y
                 for i in range(8):
                     mr, mi = mats[two, f, 0, i], mats[two, f, 1, i]
-                    own = pick(share, sub8 + 16 * i)
                     vr = jnp.sum(mr * yr - mi * yi, axis=1, keepdims=True)
                     vi = jnp.sum(mr * yi + mi * yr, axis=1, keepdims=True)
-                    state[f, 0, i] = own * vr
-                    state[f, 1, i] = own * vi
+                    state[f, 0, i] = jnp.broadcast_to(vr, small)
+                    state[f, 1, i] = jnp.broadcast_to(vi, small)
             return carry
 
         lax.fori_loop(0, pairs_of(way), step, 0)
@@ -587,8 +610,11 @@
             out += [br * tr - bi * ti, br * ti + bi * tr]
         return out
 
-    send_feed(fx, fxr, fmsg, d + 1, nd)
+    send_feed(0, fx, fxr, fmsg)
+    await_bytes(tr.at[pl.ds(0, nd - 1)], trr)
+    await_blocks(0, gr, grr)
     build_all(0)
+    await_blocks(0, fr, frr)
     sweep(0)
     weak = radiate(0)
     flow = []
@@ -604,6 +630,7 @@
     for copy in halo2:
         copy.start()
 
+    await_blocks(1, gr, grr)
     build_all(1)
     for copy in halo2:
         copy.wait_recv()
@@ -618,7 +645,8 @@
         driven[2 * f] = dr
         driven[2 * f + 1] = di
     project(1, driven, fx2, fxs2, fxr2)
-    send_feed(fx2, fxr2, fmsg2, 0, d)
+    send_feed(1, fx2, fxr2, fmsg2)
+    await_blocks(1, fr, frr)
     sweep(1)
     weak = radiate(1)
     for f in range(F):
@@ -633,6 +661,7 @@
     await_bytes(fx2.at[pl.ds(0, nx - 1)], fxs2)
     await_bytes(gr.at[pl.ds(0, nd - 1)], grs)
     await_bytes(fr.at[pl.ds(0, nd - 1)], frs)
+    await_bytes(tr.at[pl.ds(0, nd - 1)], trs)
 
 
 def solution(mesh):
@@ -641,12 +670,15 @@
 
     def per_device(incident, inverse_diag, previous, heights, neighbours, counts, transmit, angle_weights):
         vmem = pl.BlockSpec(memory_space=pltpu.VMEM)
-        anywhere = pl.BlockSpec(memory_space=pl.ANY)
+        far = pl.BlockSpec(memory_space=pltpu.HBM)
         points = RD * XD
         block = jax.ShapeDtypeStruct((2 * F, RD, XD), f32)
         V = pltpu.VMEM
         dma = pltpu.SemaphoreType.DMA
-        scratch = [
+        held = [V(a.shape, a.dtype) for a in (
+            incident, inverse_diag, previous, heights, neighbours, counts, transmit, angle_weights, v_rows
+        )]
+        scratch = held + [
             V((RD, 2, 16, XD), f32), V((12, RD, XD), f32),
             V((5, 32, XD), f32), V((32, XD), f32), V((32, XD), f32), V((RD, XD), f32), V((RD, XD), f32),
             V((4, 32, XD), f32), V((32, XD), f32), V((32, XD), f32), V((RD, XD), f32), V((RD, XD), f32),
@@ -654,22 +686,22 @@
             V((64, points), bf16), V((64, points), bf16), V((64, points), bf16), V((64, points), bf16),
             V((2, 8, points), f32), V((32, points), bf16), V((32, points), bf16),
             V((4, RD, XD), f32), V((4, RD, XD), f32), V((4, RD, XD), f32), V((4, RD, XD), f32),
-            V((4, 8, 128), f32), V((4, 8, 8, 128), f32), V((8, 128), f32),
+            V((4, 8, 128), f32), V((4, 8, 8, 128), f32), V((8, 128), f32), V((2, 128), f32), V((nd + 2, 2, 128), f32),
             V((nx, 16, 128), f32), V((2, 8, 128), f32), V((nd + 2, 8, 128), f32),
-            V((nx, 8, 128), f32), V((nx, 8, 128), f32), V((8, 128), f32), V((8, 128), f32),
-            V((nd + 2, 8, 128), f32), V((nd + 2, F, 2, 8, 8, 128), f32), V((F, 2, 8, 8, 128), f32),
+            V((nx, 4, 128), f32), V((nx, 4, 128), f32), V((4, 128), f32), V((4, 128), f32),
+            V((nd + 2, 4, 128), f32), V((nd + 2, F, 2, 8, 8, 128), f32), V((F, 2, 8, 8, 128), f32),
             V((8, RD, XD), f32), V((6, RD, XD), f32),
-            dma((2,)), dma((8,)), dma((8,)), dma((8,)), dma((8,)),
-            dma, dma, dma, dma((nd,)), dma, dma, dma, dma, dma, dma((nd,)),
+            dma((11,)), dma((8,)), dma((8,)), dma((8,)), dma((8,)),
+            dma, dma, dma, dma((nd,)), dma, dma, dma, dma, dma, dma((nd,)), dma, dma,
         ]
         return pl.pallas_call(
             functools.partial(kernel, nd, nx),
             out_shape=(block, block),
-            in_specs=[vmem] * 9 + [anywhere] * 2,
+            in_specs=[far] * 11,
             out_specs=(vmem, vmem),
             scratch_shapes=scratch,
             compiler_params=pltpu.CompilerParams(
-                collective_id=0, has_side_effects=True, vmem_limit_bytes=40 << 20
+                collective_id=0, has_side_effects=True, vmem_limit_bytes=60 << 20
             ),
         )(
             incident, inverse_diag, previous, heights, neighbours, counts, transmit, angle_weights,

time: 74.6 us -> 58.2 us (0.78)
  local copies, waits for them, and re-layouts: 10.1 us -> 2 us
  Pallas kernels: 63.2 us -> 55.3 us
    unnamed x24 -> x4, local copies, waits for them, and re-layouts: 10.1 us -> 2 us
    pallas_call x1, Pallas kernels: 63.2 us -> 55.3 us  [per_device(): pl.pallas_call(functools.partial(kernel, nd, nx), out_shape=(block, block...]
where the time goes in v2:
time: 58.2 us; the launch traced here: 58 us
  Pallas kernels  55.3 us (95%)
  local copies, waits for them, and re-layouts  2 us (3%)
  between operations  0.65 us (1%)
    pallas_call x1, Pallas kernels, per_device(): pl.pallas_call(functools.partial(kernel, nd, nx), out_shape=(block, block...  55.3 us
    unnamed x4, local copies, waits for them, and re-layouts  2 us

profile of v2, /device:TPU:1, one launch (start us, length us, event | category | flops | bytes accessed | tf_op | source)
XLA Modules:
  0.0 58.0 jit_solution(9197140067484316760)
XLA Ops:
  0.6 55.3 %shard_map.122 = (f32[4,16,128]{2,1,0:T(8,128)}, f32[4,16,128]{2,1,0:T(8,128)}) custom-call(f32[4,16,128]{2,1,0:T(8,128)} %inc_hbm.1, f32[4,16,128]{2,1,0:T(8,128)} %zin_hbm.1, f32[4,16,128]{2,1,0:T(8,128)} %prev_hbm.1, f32[16,128]{1,0:T(8,128)} %hts_hbm.1, s32[24,16,128]{2,1,0:T(8,128)} %nbr_hbm.1, s32[16,128]{1,0:T(8,128)} %cnt_hbm.1, ...), custom_call_target="tpu_custom_call" | custom-call | tf_op jit(solution)/shard_map/pallas_call | solution.py:697
  56.0 0.0 copy-start
  56.0 1.4 %copy.15 = f32[4,16,128]{2,1,0:T(8,128)} copy(f32[4,16,128]{2,1,0:T(8,128)} %get-tuple-element.4) | data formatting | bytes 65536
  57.4 0.0 copy-done
  57.4 0.6 %copy.16 = f32[4,16,128]{2,1,0:T(8,128)} copy(f32[4,16,128]{2,1,0:T(8,128)S(1)} %copy-done) | data formatting | bytes 65536
Async XLA Ops:
  56.0 1.4 %copy-start = (f32[4,16,128]{2,1,0:T(8,128)S(1)}, f32[4,16,128]{2,1,0:T(8,128)}, u32[]{:S(2)}) copy-start(f32[4,16,128]{2,1,0:T(8,128)} %get-tuple-element.5) | copy-start | bytes 98308

commit v3 on v2

--- a/solution.py
+++ b/solution.py
@@ -44,7 +44,20 @@
         cell[dm, 8], cell[dm, 9] = np.cos(ang), np.sin(ang)
         ang = turn * ((0 * rows[:, None] + cols[None, :]) % 64)
         cell[dm, 10], cell[dm, 11] = np.cos(ang), np.sin(ang)
-    return v_rows, u_rows, cell
+    lane = np.arange(XD)
+    side = np.where(lane < 8, lane - 3, lane + 120)
+    wide = np.zeros((4, 8, 4, RD, XD), np.float32)
+    for dm in range(4):
+        rows = 16 * dm - 8 + np.arange(32)
+        row_at = np.stack([np.r_[rows[:8], rows[:8]], rows[8:24], rows[8:24], np.r_[rows[24:], rows[24:]]])
+        half = np.concatenate([np.tile(lane, (8, 1)), np.tile(side, (8, 1))])
+        col_at = np.stack([half, np.tile(lane, (RD, 1)), np.tile(side, (RD, 1)), half])
+        row_at = row_at[:, :, None] + 0 * col_at
+        angs = [(1 + 2 * f) * row_at + (f - 4) * col_at for f in range(F)] + [row_at, col_at]
+        for n, ang in enumerate(angs):
+            wide[dm, 2 * n] = np.cos(turn * (ang % 64))
+            wide[dm, 2 * n + 1] = np.sin(turn * (ang % 64))
+    return v_rows, u_rows, cell, wide
 
 
 def sincos_small(t):
@@ -123,9 +136,9 @@
 
 def kernel(
     nd, nx,
-    inc_hbm, zin_hbm, prev_hbm, hts_hbm, nbr_hbm, cnt_hbm, trn_hbm, aw_hbm, v_hbm, u_hbm, cell_hbm,
+    inc_hbm, zin_hbm, prev_hbm, hts_hbm, nbr_hbm, cnt_hbm, trn_hbm, aw_hbm, v_hbm, u_hbm, cell_hbm, wide_hbm,
     out_f, out_c,
-    inc, zin, prev, hts, nbr, cnt, trn, aw, v_rows, u_rows, cell, cbuf, edge_l, edge_r, pk_l, pk_r,
+    inc, zin, prev, hts, nbr, cnt, trn, aw, v_rows, u_rows, cell, wide_cell, pz, psrc, pwave, cflow, eflow, near_rows, cbuf, edge_l, edge_r, pk_l, pk_r,
     cbuf2, edge_l2, edge_r2, pk_l2, pk_r2,
     shifted, table, tab_u_h, tab_u_l, tab_a_h, tab_a_l, tab_v, tab_f_h, tab_f_l,
     srcp, loaded, driven, weakf, w_lane, w_sub, row_buf, share_msg, tr,
@@ -163,8 +176,9 @@
         pl.semaphore_signal(barrier, inc=1, device_id=peer, device_id_type=MESH)
 
     fetches = [
-        (prev_hbm, prev), (hts_hbm, hts), (trn_hbm, trn), (v_hbm, v_rows), (u_hbm.at[dm], u_rows), (zin_hbm, zin),
+        (prev_hbm, prev), (hts_hbm, hts), (zin_hbm, zin), (trn_hbm, trn), (v_hbm, v_rows), (u_hbm.at[dm], u_rows),
         (aw_hbm, aw), (cell_hbm.at[dm], cell), (cnt_hbm, cnt), (nbr_hbm, nbr), (inc_hbm, inc),
+        (wide_hbm.at[dm], wide_cell),
     ]
     fetches = [pltpu.make_async_copy(a, b, csem.at[n]) for n, (a, b) in enumerate(fetches)]
     for fetch in fetches:
@@ -186,23 +200,25 @@
         to_left[...] = a
         to_right[...] = b
 
-    for fetch in fetches[:2]:
+    for fetch in fetches[:3]:
         fetch.wait()
     for c in range(4):
         cbuf[c, 8:24, :] = prev[c]
+        cbuf[5 + c, 8:24, :] = zin[c]
     cbuf[4, 8:24, :] = hts[...]
-    pack_edges([prev[0], prev[1], prev[2], prev[3], hts[...]], pk_l, pk_r)
+    pack_edges([prev[c] for c in range(4)] + [hts[...]] + [zin[c] for c in range(4)], pk_l, pk_r)
     zero8 = jnp.zeros(small, f32)
     li, lj = lane8 // 16, lane8 % 16
     for slot in (0, nd + 1):
         gr[slot] = zero8
         fr[slot] = jnp.zeros((4, 128), f32)
         tr[slot] = jnp.zeros((2, 128), f32)
-    fetches[2].wait()
+    fetches[3].wait()
     row_buf[...] = zero8
     row_buf[4:6, 0:Q] = trn[0]
     share_rows = jnp.where(lj < 8, pick(row_buf[...], (li * 8 + lj) & 127), 0.0)
     share_msg[...] = share_rows[4:6, :]
+    tr[d + 1] = share_rows[4:6, :]
 
     pl.semaphore_wait(barrier, nd - 1 + nx - 1 + 4)
 
@@ -234,7 +250,7 @@
             device_id=(to, x), device_id_type=MESH,
         ).start()
 
-    for fetch in fetches[3:6]:
+    for fetch in fetches[4:6]:
         fetch.wait()
     power16 = (rows_of(wide) - 7).astype(f32) * 0.03
 
@@ -333,23 +349,39 @@
     row32 = rows_of(tall) + (d * RD - 8)
     inside = (row32 >= 0) & (row32 < nd * RD)
 
-    def shift_all(buf, e_l, e_r, count):
-        el = jnp.where(inside & (lane32 < 128 * x), e_l[...], 0.0)
-        er = jnp.where(inside & (lane32 < 128 * (nx - 1 - x)), e_r[...], 0.0)
+    def shift_all(buf, edges, count):
+        to_left = inside & (lane32 < 128 * x)
+        to_right = inside & (lane32 < 128 * (nx - 1 - x))
         for c in range(count):
+            el, left_at, er, right_at = edges(c)
+            el = jnp.where(to_left, el, 0.0)
+            er = jnp.where(to_right, er, 0.0)
             mid = jnp.where(inside, buf[c], 0.0)
             shifted[H, c] = mid
             for k in range(1, H + 1):
                 shifted[H + k, c] = jnp.where(
                     lane32 >= 128 - k,
-                    pltpu.roll(er, (128 - k - 8 * c) % 128, 1),
+                    pltpu.roll(er, (128 - k - right_at) % 128, 1),
                     pltpu.roll(mid, 128 - k, 1),
                 )
                 shifted[H - k, c] = jnp.where(
                     lane32 < k,
-                    pltpu.roll(el, (k - 3 - 8 * c) % 128, 1),
+                    pltpu.roll(el, (k - 3 - left_at) % 128, 1),
                     pltpu.roll(mid, k, 1),
                 )
+
+    def sides(e_l, e_r, c):
+        left_part = e_l[...] if c == 0 else pltpu.roll(e_l[...], 128 - 8 * c, 1)
+        right_part = e_r[...] if c == 1 else pltpu.roll(e_r[...], (136 - 8 * c) % 128, 1)
+        return jnp.where(lane32 < 8, left_part, right_part)
+
+    def grouped(center, edge):
+        return (
+            jnp.concatenate([center[:8], edge[:8]], axis=0),
+            center[8:24],
+            edge[8:24],
+            jnp.concatenate([center[24:], edge[24:]], axis=0),
+        )
 
     def window(dyi, c, dx):
         return shifted[dyi, c, 8 + dx : 24 + dx, :]
@@ -365,7 +397,7 @@
 
     for copy in halo1:
         copy.wait_recv()
-    shift_all(cbuf, edge_l, edge_r, 5)
+    shift_all(cbuf, lambda c: (edge_l[...], 8 * c, edge_r[...], 8 * c), 5)
 
     def couple(dyi, total):
         dy = dyi - H
@@ -444,6 +476,28 @@
         loaded[2 * f] = sr
         loaded[2 * f + 1] = si
     project(0, loaded, fx, fxs, fxr)
+    for c in range(4):
+        cbuf2[c, 8:24, :] = loaded[c]
+    pack_edges([loaded[c] for c in range(4)], pk_l2, pk_r2)
+    halo2 = halo(cbuf2, edge_l2, edge_r2, pk_l2, pk_r2, hs2_sem, hr2_sem)
+    for copy in halo2:
+        copy.start()
+
+    for g, height in enumerate(grouped(cbuf[4], sides(edge_l, edge_r, 4))):
+        hs, hc = sincos_small(0.03 * height)
+        c8, s8 = squared(*squared(*squared(hc, hs)))
+        pwave[4, g] = c8 * wide_cell[4, g] - s8 * wide_cell[5, g]
+        pwave[5, g] = s8 * wide_cell[4, g] + c8 * wide_cell[5, g]
+        pwave[6, g] = hc * wide_cell[6, g] - hs * wide_cell[7, g]
+        pwave[7, g] = hc * wide_cell[7, g] + hs * wide_cell[6, g]
+        for f in range(F):
+            k = 2 * f
+            s, c = sincos((0.3 + 0.2 * f) * height)
+            pwave[k, g] = c * wide_cell[k, g] - s * wide_cell[k + 1, g]
+            pwave[k + 1, g] = s * wide_cell[k, g] + c * wide_cell[k + 1, g]
+    for c in range(4):
+        for g, value in enumerate(grouped(cbuf[5 + c], sides(edge_l, edge_r, 5 + c))):
+            pz[c, g] = value
 
     await_bytes(gx.at[pl.ds(0, nx - 1)], gxr)
     g_sum = total_xr(gx)
@@ -458,9 +512,13 @@
             device_id=(to, x), device_id_type=MESH,
         ).start()
 
+    gr[d + 1] = gmsg[0]
+
     def send_feed(way, buf, recv, msg):
         await_bytes(buf.at[pl.ds(0, nx - 1)], recv)
         msg[...] = total_xr(buf)
+        if way == 0:
+            fr[d + 1] = msg[...]
         for to in blocks:
 
             @pl.when(to < d if way else to > d)
@@ -538,31 +596,37 @@
 
         lax.fori_loop(0, pairs_of(way), step, 0)
 
+    def tree(terms):
+        while len(terms) > 1:
+            terms = [a + b for a, b in zip(terms[::2], terms[1::2])]
+        return terms[0]
+
+    def carry_rows(one, f):
+        real, imag = [], []
+        for i in range(8):
+            mr, mi = mats[one, f, 0, i], mats[one, f, 1, i]
+            sr, si = state[1, f, 0, i], state[1, f, 1, i]
+            real.append(mr * sr - mi * si)
+            imag.append(mr * si + mi * sr)
+        share = tr[one, f : f + 1, :]
+        return [
+            share * (jnp.sum(tree(terms), axis=0, keepdims=True) + fr[one, 2 * f + c : 2 * f + c + 1, :])
+            for c, terms in enumerate((real, imag))
+        ]
+
     def sweep(way):
         for f in range(F):
             for c in range(2):
                 for i in range(8):
-                    state[f, c, i] = zero8
-
-        def tree(terms):
-            while len(terms) > 1:
-                terms = [a + b for a, b in zip(terms[::2], terms[1::2])]
-            return terms[0]
+                    state[1, f, c, i] = zero8
 
         def step(t, carry):
             one, two = slots_of(way, t)
             for f in range(F):
-                tr_, ti_ = [], []
-                for i in range(8):
-                    mr, mi = mats[one, f, 0, i], mats[one, f, 1, i]
-                    sr, si = state[f, 0, i], state[f, 1, i]
-                    tr_.append(mr * sr - mi * si)
-                    ti_.append(mr * si + mi * sr)
-                share = tr[one, f : f + 1, :]
                 y = []
-                for c, terms in enumerate((tr_, ti_)):
+                for c, row in enumerate(carry_rows(one, f)):
                     k = 2 * f + c
-                    row = share * (jnp.sum(tree(terms), axis=0, keepdims=True) + fr[one, k : k + 1, :])
+                    near_rows[k : k + 1, :] = row
                     row = row + jnp.where(lj[:1] < 8, 0.0, fr[two, k : k + 1, :])
                     y.append(jnp.broadcast_to(row, small))
                 yr, yi = y
@@ -570,21 +634,35 @@
                     mr, mi = mats[two, f, 0, i], mats[two, f, 1, i]
                     vr = jnp.sum(mr * yr - mi * yi, axis=1, keepdims=True)
                     vi = jnp.sum(mr * yi + mi * yr, axis=1, keepdims=True)
-                    state[f, 0, i] = jnp.broadcast_to(vr, small)
-                    state[f, 1, i] = jnp.broadcast_to(vi, small)
+                    state[1, f, 0, i] = jnp.broadcast_to(vr, small)
+                    state[1, f, 1, i] = jnp.broadcast_to(vi, small)
             return carry
 
         lax.fori_loop(0, pairs_of(way), step, 0)
 
-    def radiate(way):
+    def neighbour_carries():
+        before = [jnp.broadcast_to(near_rows[k : k + 1, :], small) for k in range(4)]
+        after = []
+        for f in range(F):
+            after += [jnp.broadcast_to(row, small) for row in carry_rows(d + 1, f)]
+        for i in range(8):
+            index = sub8 + 16 * i
+            for f in range(F):
+                for c in range(2):
+                    state[0, f, c, i] = pick(before[2 * f + c], index)
+                    state[2, f, c, i] = pick(after[2 * f + c], index)
+
+    def weigh(which):
         for f in range(F):
             for i in range(8):
                 wr, wi = w_sub[2 * f, i], w_sub[2 * f + 1, i]
-                sr, si = state[f, 0, i], state[f, 1, i]
-                state[f, 0, i] = wr * sr - wi * si
-                state[f, 1, i] = wr * si + wi * sr
-        vr, vi = vu[0], vu[1]
-        ur, ui = vu[2 + 2 * way], vu[3 + 2 * way]
+                sr, si = state[which, f, 0, i], state[which, f, 1, i]
+                state[which, f, 0, i] = wr * sr - wi * si
+                state[which, f, 1, i] = wr * si + wi * sr
+
+    def radiate(which, v, u, bases):
+        vr, vi = v
+        ur, ui = u
 
         def step(n, total):
             i = 7 - n
@@ -593,7 +671,7 @@
                 tr, ti = total[2 * f], total[2 * f + 1]
 
                 def coef(c, j):
-                    return jnp.broadcast_to(state[f, c, i, j : j + 1, :], wide)
+                    return jnp.broadcast_to(state[which, f, c, i, j : j + 1, :], wide)
 
                 ar, ai = coef(0, 7), coef(1, 7)
                 for j in range(6, -1, -1):
@@ -604,8 +682,7 @@
         total = lax.fori_loop(0, 8, step, nothing)
         out = []
         for f in range(F):
-            k = way * 4 + f * 2
-            br, bi = base[k], base[k + 1]
+            br, bi = bases[2 * f], bases[2 * f + 1]
             tr, ti = total[2 * f], total[2 * f + 1]
             out += [br * tr - bi * ti, br * ti + bi * tr]
         return out
@@ -614,27 +691,42 @@
     await_bytes(tr.at[pl.ds(0, nd - 1)], trr)
     await_blocks(0, gr, grr)
     build_all(0)
+    build(d + 1, True)
+    await_blocks(1, gr, grr)
+    build_all(1)
+    near_rows[...] = jnp.zeros((4, 128), f32)
+    for copy in halo2:
+        copy.wait_recv()
+    for c in range(4):
+        for g, value in enumerate(grouped(cbuf2[c], sides(edge_l2, edge_r2, c))):
+            psrc[c, g] = value
     await_blocks(0, fr, frr)
     sweep(0)
-    weak = radiate(0)
-    flow = []
-    for f in range(F):
-        ar, ai = times_z(f, weak[2 * f], weak[2 * f + 1])
-        flow += [loaded[2 * f] - ar, loaded[2 * f + 1] - ai]
-    for c in range(4):
-        out_f[c] = flow[c]
-        cbuf2[c, 8:24, :] = flow[c]
-        weakf[c] = weak[c]
-    pack_edges(flow, pk_l2, pk_r2)
-    halo2 = halo(cbuf2, edge_l2, edge_r2, pk_l2, pk_r2, hs2_sem, hr2_sem)
-    for copy in halo2:
-        copy.start()
-
-    await_blocks(1, gr, grr)
-    build_all(1)
-    for copy in halo2:
-        copy.wait_recv()
-    shift_all(cbuf2, edge_l2, edge_r2, 4)
+    neighbour_carries()
+    for which in range(3):
+        weigh(which)
+    for g in range(4):
+        weak = radiate(
+            (g + 1) // 2, (pwave[6, g], pwave[7, g]), (pwave[4, g], pwave[5, g]), [pwave[k, g] for k in range(4)]
+        )
+        for f in range(F):
+            zr, zi = pz[2 * f, g], pz[2 * f + 1, g]
+            wr, wi = weak[2 * f], weak[2 * f + 1]
+            for c, flow in (
+                (2 * f, psrc[2 * f, g] - (zr * wr - zi * wi)),
+                (2 * f + 1, psrc[2 * f + 1, g] - (zr * wi + zi * wr)),
+            ):
+                if g == 1:
+                    out_f[c] = flow
+                    weakf[c] = weak[c]
+                    cflow[c, 8:24, :] = flow
+                elif g == 2:
+                    eflow[c, 8:24, :] = flow
+                else:
+                    at = slice(0, 8) if g == 0 else slice(24, 32)
+                    cflow[c, at, :] = flow[:8]
+                    eflow[c, at, :] = flow[8:]
+    shift_all(cflow, lambda c: (eflow[c], 0, eflow[c], 8), 4)
     near_new = lax.fori_loop(0, SIDE, recouple, nothing)
     for f in range(F):
         dr, di = times_z(
@@ -648,7 +740,8 @@
     send_feed(1, fx2, fxr2, fmsg2)
     await_blocks(1, fr, frr)
     sweep(1)
-    weak = radiate(1)
+    weigh(1)
+    weak = radiate(1, (vu[0], vu[1]), (vu[4], vu[5]), [base[4 + k] for k in range(4)])
     for f in range(F):
         ar, ai = times_z(f, weak[2 * f], weak[2 * f + 1])
         out_c[2 * f] = driven[2 * f] - ar
@@ -666,13 +759,12 @@
 
 def solution(mesh):
     nd, nx = mesh.shape["rng"], mesh.shape["xr"]
-    v_rows, u_rows, cell = phase_tables()
+    v_rows, u_rows, cell, wide = phase_tables()
 
     def per_device(incident, inverse_diag, previous, heights, neighbours, counts, transmit, angle_weights):
         vmem = pl.BlockSpec(memory_space=pltpu.VMEM)
         far = pl.BlockSpec(memory_space=pltpu.HBM)
         points = RD * XD
-        block = jax.ShapeDtypeStruct((2 * F, RD, XD), f32)
         V = pltpu.VMEM
         dma = pltpu.SemaphoreType.DMA
         held = [V(a.shape, a.dtype) for a in (
@@ -680,7 +772,9 @@
         )]
         scratch = held + [
             V((RD, 2, 16, XD), f32), V((12, RD, XD), f32),
-            V((5, 32, XD), f32), V((32, XD), f32), V((32, XD), f32), V((RD, XD), f32), V((RD, XD), f32),
+            V((8, 4, RD, XD), f32), V((4, 4, RD, XD), f32), V((4, 4, RD, XD), f32), V((8, 4, RD, XD), f32),
+            V((4, 32, XD), f32), V((4, 32, XD), f32), V((4, 128), f32),
+            V((9, 32, XD), f32), V((32, XD), f32), V((32, XD), f32), V((RD, XD), f32), V((RD, XD), f32),
             V((4, 32, XD), f32), V((32, XD), f32), V((32, XD), f32), V((RD, XD), f32), V((RD, XD), f32),
             V((SIDE, 5, 32, XD), f32), V((SIDE, SIDE, 4, RD, XD), f32),
             V((64, points), bf16), V((64, points), bf16), V((64, points), bf16), V((64, points), bf16),
@@ -689,15 +783,15 @@
             V((4, 8, 128), f32), V((4, 8, 8, 128), f32), V((8, 128), f32), V((2, 128), f32), V((nd + 2, 2, 128), f32),
             V((nx, 16, 128), f32), V((2, 8, 128), f32), V((nd + 2, 8, 128), f32),
             V((nx, 4, 128), f32), V((nx, 4, 128), f32), V((4, 128), f32), V((4, 128), f32),
-            V((nd + 2, 4, 128), f32), V((nd + 2, F, 2, 8, 8, 128), f32), V((F, 2, 8, 8, 128), f32),
+            V((nd + 2, 4, 128), f32), V((nd + 2, F, 2, 8, 8, 128), f32), V((3, F, 2, 8, 8, 128), f32),
             V((8, RD, XD), f32), V((6, RD, XD), f32),
-            dma((11,)), dma((8,)), dma((8,)), dma((8,)), dma((8,)),
+            dma((12,)), dma((8,)), dma((8,)), dma((8,)), dma((8,)),
             dma, dma, dma, dma((nd,)), dma, dma, dma, dma, dma, dma((nd,)), dma, dma,
         ]
         return pl.pallas_call(
             functools.partial(kernel, nd, nx),
-            out_shape=(block, block),
-            in_specs=[far] * 11,
+            out_shape=(V((2 * F, RD, XD), f32), V((2 * F, RD, XD), f32)),
+            in_specs=[far] * 12,
             out_specs=(vmem, vmem),
             scratch_shapes=scratch,
             compiler_params=pltpu.CompilerParams(
@@ -705,7 +799,7 @@
             ),
         )(
             incident, inverse_diag, previous, heights, neighbours, counts, transmit, angle_weights,
-            jnp.asarray(v_rows), jnp.asarray(u_rows), jnp.asarray(cell),
+            jnp.asarray(v_rows), jnp.asarray(u_rows), jnp.asarray(cell), jnp.asarray(wide),
         )
 
     placed = (

time: 58.2 us -> 55.4 us (0.952)
  Pallas kernels: 55.3 us -> 53.4 us
  local copies, waits for them, and re-layouts: 2 us -> 1.23 us
    pallas_call x1, Pallas kernels: 55.3 us -> 53.4 us  [per_device(): pl.pallas_call(functools.partial(kernel, nd, nx), out_shape=(V((2 * F, RD...]
    unnamed x4 -> x2, local copies, waits for them, and re-layouts: 2 us -> 1.23 us
where the time goes in v3:
time: 55.4 us; the launch traced here: 55.3 us
  Pallas kernels  53.4 us (96%)
  local copies, waits for them, and re-layouts  1.23 us (2%)
  between operations  0.64 us (1%)
    pallas_call x1, Pallas kernels, per_device(): pl.pallas_call(functools.partial(kernel, nd, nx), out_shape=(V((2 * F, RD...  53.4 us
    unnamed x2, local copies, waits for them, and re-layouts  1.23 us

profile of v3, /device:TPU:1, one launch (start us, length us, event | category | flops | bytes accessed | tf_op | source)
XLA Modules:
  0.0 55.3 jit_solution(9468417142830529798)
XLA Ops:
  0.6 53.4 %shard_map.131 = (f32[4,16,128]{2,1,0:T(8,128)S(1)}, f32[4,16,128]{2,1,0:T(8,128)S(1)}) custom-call(f32[4,16,128]{2,1,0:T(8,128)} %inc_hbm.1, f32[4,16,128]{2,1,0:T(8,128)} %zin_hbm.1, f32[4,16,128]{2,1,0:T(8,128)} %prev_hbm.1, f32[16,128]{1,0:T(8,128)} %hts_hbm.1, s32[24,16,128]{2,1,0:T(8,128)} %nbr_hbm.1, s32[16,128]{1,0:T(8,128)} %cnt_hbm.1, ...), custom_call_target="tpu_custom_call" | custom-call | tf_op jit(solution)/shard_map/pallas_call | solution.py:791
  54.0 0.6 %copy.16 = f32[4,16,128]{2,1,0:T(8,128)} copy(f32[4,16,128]{2,1,0:T(8,128)S(1)} %get-tuple-element.2) | data formatting | bytes 65536
  54.6 0.6 %copy.17 = f32[4,16,128]{2,1,0:T(8,128)} copy(f32[4,16,128]{2,1,0:T(8,128)S(1)} %get-tuple-element.3) | data formatting | bytes 65536

commit v4 on v3

--- a/solution.py
+++ b/solution.py
@@ -141,7 +141,7 @@
     inc, zin, prev, hts, nbr, cnt, trn, aw, v_rows, u_rows, cell, wide_cell, pz, psrc, pwave, cflow, eflow, near_rows, cbuf, edge_l, edge_r, pk_l, pk_r,
     cbuf2, edge_l2, edge_r2, pk_l2, pk_r2,
     shifted, table, tab_u_h, tab_u_l, tab_a_h, tab_a_l, tab_v, tab_f_h, tab_f_l,
-    srcp, loaded, driven, weakf, w_lane, w_sub, row_buf, share_msg, tr,
+    srcp, loaded, driven, weakf, w_lane, w_sub, row_buf, share_msg, tr, tb,
     gx, gmsg, gr, fx, fx2, fmsg, fmsg2, fr, mats, state,
     base, vu,
     csem, hs_sem, hr_sem, hs2_sem, hr2_sem,
@@ -220,8 +220,6 @@
     share_msg[...] = share_rows[4:6, :]
     tr[d + 1] = share_rows[4:6, :]
 
-    pl.semaphore_wait(barrier, nd - 1 + nx - 1 + 4)
-
     def halo(buf, e_l, e_r, p_l, p_r, send, recv):
         plan = [
             (p_l.at[0:8, :], e_r.at[24:32, :], (up, left)),
@@ -240,15 +238,6 @@
             )
             for n, (src, dst, dev) in enumerate(plan)
         ]
-
-    halo1 = halo(cbuf, edge_l, edge_r, pk_l, pk_r, hs_sem, hr_sem)
-    for copy in halo1:
-        copy.start()
-    for to in blocks:
-        pltpu.make_async_remote_copy(
-            src_ref=share_msg, dst_ref=tr.at[d + 1], send_sem=trs, recv_sem=trr,
-            device_id=(to, x), device_id_type=MESH,
-        ).start()
 
     for fetch in fetches[4:6]:
         fetch.wait()
@@ -303,6 +292,15 @@
             total = total + buf[k]
         return total
 
+    pl.semaphore_wait(barrier, nd - 1 + nx - 1 + 4)
+    halo1 = halo(cbuf, edge_l, edge_r, pk_l, pk_r, hs_sem, hr_sem)
+    for copy in halo1:
+        copy.start()
+    for to in blocks:
+        pltpu.make_async_remote_copy(
+            src_ref=share_msg, dst_ref=tr.at[d + 1], send_sem=trs, recv_sem=trr,
+            device_id=(to, x), device_id_type=MESH,
+        ).start()
     spread_xr(gx, gxs, gxr)
 
     for fetch in fetches[6:]:
@@ -476,6 +474,21 @@
         loaded[2 * f] = sr
         loaded[2 * f + 1] = si
     project(0, loaded, fx, fxs, fxr)
+    await_bytes(gx.at[pl.ds(0, nx - 1)], gxr)
+    g_sum = total_xr(gx)
+    h0, h1 = regroup(g_sum[:8]), regroup(g_sum[8:])
+    gmsg[0] = jnp.where(sub8 < 4, h0, pltpu.roll(h1, 4, 0))
+    gmsg[1] = jnp.where(sub8 < 4, pltpu.roll(h0, 4, 0), h1)
+
+    for to in blocks:
+        pltpu.make_async_remote_copy(
+            src_ref=gmsg.at[(to < d).astype(i32)], dst_ref=gr.at[d + 1],
+            send_sem=grs, recv_sem=grr.at[d],
+            device_id=(to, x), device_id_type=MESH,
+        ).start()
+
+    gr[d + 1] = gmsg[0]
+
     for c in range(4):
         cbuf2[c, 8:24, :] = loaded[c]
     pack_edges([loaded[c] for c in range(4)], pk_l2, pk_r2)
@@ -499,20 +512,19 @@
         for g, value in enumerate(grouped(cbuf[5 + c], sides(edge_l, edge_r, 5 + c))):
             pz[c, g] = value
 
-    await_bytes(gx.at[pl.ds(0, nx - 1)], gxr)
-    g_sum = total_xr(gx)
-    h0, h1 = regroup(g_sum[:8]), regroup(g_sum[8:])
-    gmsg[0] = jnp.where(sub8 < 4, h0, pltpu.roll(h1, 4, 0))
-    gmsg[1] = jnp.where(sub8 < 4, pltpu.roll(h0, 4, 0), h1)
-
-    for to in blocks:
-        pltpu.make_async_remote_copy(
-            src_ref=gmsg.at[(to < d).astype(i32)], dst_ref=gr.at[d + 1],
-            send_sem=grs, recv_sem=grr.at[d],
-            device_id=(to, x), device_id_type=MESH,
-        ).start()
-
-    gr[d + 1] = gmsg[0]
+    await_bytes(tr.at[pl.ds(0, nd - 1)], trr)
+
+    def spread_shares(n, carry):
+        for k in range(4):
+            slot = 4 * n + (k + 1)
+            index = (lane8 & 7) * 16 + sub8
+            two = [pick(jnp.broadcast_to(tr[slot, f : f + 1, :], small), index) for f in range(F)]
+            two = jnp.where(lane8 < 8, two[0], two[1])
+            for at in range(16):
+                tb[slot, at] = jnp.broadcast_to(two[:, at : at + 1], small)
+        return carry
+
+    lax.fori_loop(0, nd // 4, spread_shares, 0)
 
     def send_feed(way, buf, recv, msg):
         await_bytes(buf.at[pl.ds(0, nx - 1)], recv)
@@ -544,10 +556,6 @@
             [jnp.broadcast_to(gr[slot, r : r + 1, :], small) for r in (k, 4 + k)]
             for k in range(4)
         ]
-        if not first:
-            index = (lane8 & 7) * 16 + sub8
-            shares = [pick(jnp.broadcast_to(tr[slot, f : f + 1, :], small), index) for f in range(F)]
-            shares = jnp.where(lane8 < 8, shares[0], shares[1])
         for i in range(8):
             src = start + 16 * i if first else start - 16 * i
             index = src & 127
@@ -565,8 +573,7 @@
                 real = jnp.where(own, 1.0, 0.0) - (mr * wr - mi * wi)
                 imag = -(mr * wi + mi * wr)
                 if not first:
-                    at = 8 * f + i
-                    share = jnp.broadcast_to(shares[:, at : at + 1], small)
+                    share = tb[slot, 8 * f + i]
                     real, imag = share * real, share * imag
                 mats[slot, f, 0, i] = real
                 mats[slot, f, 1, i] = imag
@@ -688,7 +695,6 @@
         return out
 
     send_feed(0, fx, fxr, fmsg)
-    await_bytes(tr.at[pl.ds(0, nd - 1)], trr)
     await_blocks(0, gr, grr)
     build_all(0)
     build(d + 1, True)
@@ -780,7 +786,7 @@
             V((64, points), bf16), V((64, points), bf16), V((64, points), bf16), V((64, points), bf16),
             V((2, 8, points), f32), V((32, points), bf16), V((32, points), bf16),
             V((4, RD, XD), f32), V((4, RD, XD), f32), V((4, RD, XD), f32), V((4, RD, XD), f32),
-            V((4, 8, 128), f32), V((4, 8, 8, 128), f32), V((8, 128), f32), V((2, 128), f32), V((nd + 2, 2, 128), f32),
+            V((4, 8, 128), f32), V((4, 8, 8, 128), f32), V((8, 128), f32), V((2, 128), f32), V((nd + 2, 2, 128), f32), V((nd + 2, 16, 8, 128), f32),
             V((nx, 16, 128), f32), V((2, 8, 128), f32), V((nd + 2, 8, 128), f32),
             V((nx, 4, 128), f32), V((nx, 4, 128), f32), V((4, 128), f32), V((4, 128), f32),
             V((nd + 2, 4, 128), f32), V((nd + 2, F, 2, 8, 8, 128), f32), V((3, F, 2, 8, 8, 128), f32),

time: 55.4 us -> 53.6 us (0.968)
  Pallas kernels: 53.4 us -> 51.6 us
    pallas_call x1, Pallas kernels: 53.4 us -> 51.6 us  [per_device(): pl.pallas_call(functools.partial(kernel, nd, nx), out_shape=(V((2 * F, RD...]
where the time goes in v4:
time: 53.6 us; the launch traced here: 53.5 us
  Pallas kernels  51.6 us (96%)
  local copies, waits for them, and re-layouts  1.23 us (2%)
  between operations  0.64 us (1%)
    pallas_call x1, Pallas kernels, per_device(): pl.pallas_call(functools.partial(kernel, nd, nx), out_shape=(V((2 * F, RD...  51.6 us
    unnamed x2, local copies, waits for them, and re-layouts  1.23 us

profile of v4, /device:TPU:1, one launch (start us, length us, event | category | flops | bytes accessed | tf_op | source)
XLA Modules:
  0.0 53.5 jit_solution(5230323709259520966)
XLA Ops:
  0.6 51.6 %shard_map.131 = (f32[4,16,128]{2,1,0:T(8,128)S(1)}, f32[4,16,128]{2,1,0:T(8,128)S(1)}) custom-call(f32[4,16,128]{2,1,0:T(8,128)} %inc_hbm.1, f32[4,16,128]{2,1,0:T(8,128)} %zin_hbm.1, f32[4,16,128]{2,1,0:T(8,128)} %prev_hbm.1, f32[16,128]{1,0:T(8,128)} %hts_hbm.1, s32[24,16,128]{2,1,0:T(8,128)} %nbr_hbm.1, s32[16,128]{1,0:T(8,128)} %cnt_hbm.1, ...), custom_call_target="tpu_custom_call" | custom-call | tf_op jit(solution)/shard_map/pallas_call | solution.py:797
  52.2 0.6 %copy.16 = f32[4,16,128]{2,1,0:T(8,128)} copy(f32[4,16,128]{2,1,0:T(8,128)S(1)} %get-tuple-element.2) | data formatting | bytes 65536
  52.8 0.6 %copy.17 = f32[4,16,128]{2,1,0:T(8,128)} copy(f32[4,16,128]{2,1,0:T(8,128)S(1)} %get-tuple-element.3) | data formatting | bytes 65536

commit v5 on v4

--- a/solution.py
+++ b/solution.py
@@ -292,17 +292,6 @@
             total = total + buf[k]
         return total
 
-    pl.semaphore_wait(barrier, nd - 1 + nx - 1 + 4)
-    halo1 = halo(cbuf, edge_l, edge_r, pk_l, pk_r, hs_sem, hr_sem)
-    for copy in halo1:
-        copy.start()
-    for to in blocks:
-        pltpu.make_async_remote_copy(
-            src_ref=share_msg, dst_ref=tr.at[d + 1], send_sem=trs, recv_sem=trr,
-            device_id=(to, x), device_id_type=MESH,
-        ).start()
-    spread_xr(gx, gxs, gxr)
-
     for fetch in fetches[6:]:
         fetch.wait()
     for f in range(F):
@@ -341,6 +330,17 @@
 
     zero_word = jnp.zeros(wide, i32)
     words = lax.fori_loop(0, LMAX, note, (zero_word, zero_word))
+
+    pl.semaphore_wait(barrier, nd - 1 + nx - 1 + 4)
+    halo1 = halo(cbuf, edge_l, edge_r, pk_l, pk_r, hs_sem, hr_sem)
+    for copy in halo1:
+        copy.start()
+    spread_xr(gx, gxs, gxr)
+    for to in blocks:
+        pltpu.make_async_remote_copy(
+            src_ref=share_msg, dst_ref=tr.at[d + 1], send_sem=trs, recv_sem=trr,
+            device_id=(to, x), device_id_type=MESH,
+        ).start()
 
     tall = (32, XD)
     lane32 = lanes_of(tall)
@@ -698,8 +698,6 @@
     await_blocks(0, gr, grr)
     build_all(0)
     build(d + 1, True)
-    await_blocks(1, gr, grr)
-    build_all(1)
     near_rows[...] = jnp.zeros((4, 128), f32)
     for copy in halo2:
         copy.wait_recv()
@@ -743,6 +741,8 @@
         driven[2 * f] = dr
         driven[2 * f + 1] = di
     project(1, driven, fx2, fxs2, fxr2)
+    await_blocks(1, gr, grr)
+    build_all(1)
     send_feed(1, fx2, fxr2, fmsg2)
     await_blocks(1, fr, frr)
     sweep(1)

time: 53.6 us -> 53.4 us (level)
  no operation moved by 1% of the time
where the time goes in v5:
time: 53.4 us; the launch traced here: 53.2 us
  Pallas kernels  51.4 us (96%)
  local copies, waits for them, and re-layouts  1.23 us (2%)
  between operations  0.64 us (1%)
    pallas_call x1, Pallas kernels, per_device(): pl.pallas_call(functools.partial(kernel, nd, nx), out_shape=(V((2 * F, RD...  51.4 us
    unnamed x2, local copies, waits for them, and re-layouts  1.23 us

profile of v5, /device:TPU:1, one launch (start us, length us, event | category | flops | bytes accessed | tf_op | source)
XLA Modules:
  0.0 53.2 jit_solution(9149225637385382560)
XLA Ops:
  0.6 51.4 %shard_map.131 = (f32[4,16,128]{2,1,0:T(8,128)S(1)}, f32[4,16,128]{2,1,0:T(8,128)S(1)}) custom-call(f32[4,16,128]{2,1,0:T(8,128)} %inc_hbm.1, f32[4,16,128]{2,1,0:T(8,128)} %zin_hbm.1, f32[4,16,128]{2,1,0:T(8,128)} %prev_hbm.1, f32[16,128]{1,0:T(8,128)} %hts_hbm.1, s32[24,16,128]{2,1,0:T(8,128)} %nbr_hbm.1, s32[16,128]{1,0:T(8,128)} %cnt_hbm.1, ...), custom_call_target="tpu_custom_call" | custom-call | tf_op jit(solution)/shard_map/pallas_call | solution.py:797
  52.0 0.6 %copy.16 = f32[4,16,128]{2,1,0:T(8,128)} copy(f32[4,16,128]{2,1,0:T(8,128)S(1)} %get-tuple-element.2) | data formatting | bytes 65536
  52.6 0.6 %copy.17 = f32[4,16,128]{2,1,0:T(8,128)} copy(f32[4,16,128]{2,1,0:T(8,128)S(1)} %get-tuple-element.3) | data formatting | bytes 65536
